TPU v7x, 512 devices: a whole 4x4x16 slice. The times are simulated.
512 devices in a mesh: island: 64 (over z, y), tensor: 8 (over x, core).
Axes of the slice: x: 4, y: 4, z: 16, core: 2. Of those that a mesh axis runs over, the one named last changes fastest.
Arguments:
- pseudo_grad: float32 [64, 128, 53248], P('island', None, 'tensor'), may hold values from -8000 to 8000
- outer_params: float32 [128, 53248], P('island', 'tensor'), may hold values from -4 to 4
- momentum: float32 [128, 53248], P('island', 'tensor'), may hold values from -6 to 6
- save_pages: int32 [64], replicated, may hold values from 1 to 208, 6656 in all
- writer: int32 [64], replicated, may hold values from 0 to 63, each once
Outputs:
- new_master: float32 [128, 53248], P('island', 'tensor')
- new_momentum: float32 [128, 53248], P('island', 'tensor')
- checkpoint: bfloat16 [64, 208, 1024], P('island', None, 'tensor')
Inputs may be any that keep to these rules, and one draw needn't show every extreme that they name: save_pages sums to 6656; the longest range has exactly 208 pages. writer names every island once.
All inputs are finite; a program needn't handle non-finite values.
Results may differ from a plain program's by a relative error of at most 0.0007.
Values may be sent and summed in bfloat16 or wider, within the bound.
No kernel may reach another device: no remote copies, remote signals or barrier semaphores. Data moves between devices by JAX's collectives and lax.ppermute only.
A program may use at most 64 MiB of HBM per device.

v0:
```python
import jax
import jax.numpy as jnp
from jax import lax
from jax.sharding import Mesh
from jax.sharding import PartitionSpec as P

ISLAND = ("island_0", "island_1")
TENSOR = ("tensor_0", "tensor_1")


epsilon = 1e-06
decay_rate = 0.9
outer_rate = 0.7


def split_up(array, dim, length):
    before, after = (array.shape[:dim], array.shape[dim + 1 :])
    return jnp.moveaxis(array.reshape(*before, length, -1, *after), dim, 0)


def sent_and_summed(array, axis, dim):
    tiles = split_up(array, dim, lax.axis_size(axis))
    arrived = lax.all_to_all(tiles, axis, split_axis=0, concat_axis=0, tiled=True)
    return arrived.sum(axis=0)


def sum_in_two_steps(array, axes, dim):
    far, near = axes
    own = sent_and_summed(split_up(array, dim, lax.axis_size(far)), near, dim + 1)
    return jnp.sum(lax.all_to_all(own, far, 0, 0, tiled=True), axis=0)


def copy_for_each(array, axis):
    length = lax.axis_size(axis)
    return lax.all_to_all(
        jnp.broadcast_to(array[None], (length, *array.shape)), axis, 0, 0, tiled=True
    )


def taken_together(array, axis):
    everything = copy_for_each(array, axis)
    return jnp.sum(everything, axis=0)


def over_axes(array, axes):
    far, near = axes
    nearer = taken_together(array, near)
    return taken_together(nearer, far)


def body(pseudo_grad, outer_params, momentum, save_pages, writer):
    own_rows = outer_params.shape[0]
    col_width = outer_params.shape[1]
    islands = lax.axis_size(ISLAND)
    my_index = lax.axis_index(ISLAND)
    own_grad = pseudo_grad[0]
    entries = own_grad.shape[0] * col_width * lax.axis_size(TENSOR)
    my_share = sum_in_two_steps(own_grad, ("island_0", "island_1"), 0)
    outer_grad = my_share / islands
    square_sum = over_axes(
        jnp.sum(outer_grad * outer_grad), (("island_0", "island_1"), ("tensor_0", "tensor_1"))
    )
    normed = outer_grad / jnp.sqrt(square_sum / entries + epsilon)
    new_momentum = decay_rate * momentum + normed
    new_master = outer_params - outer_rate * (normed + decay_rate * new_momentum)
    cast_rows = new_master.astype(jnp.bfloat16)
    pages_own = own_rows * col_width // 128
    capacity = 2 * pages_own
    starts = jnp.cumsum(save_pages) - save_pages
    targets = jnp.arange(islands, dtype=jnp.int32)
    owner_table = writer[None, :] == targets[:, None]
    range_start = jnp.sum(jnp.where(owner_table, starts[None, :], 0), axis=1)
    range_length = jnp.sum(jnp.where(owner_table, save_pages[None, :], 0), axis=1)
    is_mine = targets == my_index
    own_start = jnp.sum(jnp.where(is_mine, range_start, 0))
    own_length = jnp.sum(jnp.where(is_mine, range_length, 0))
    slot_ids = jnp.arange(capacity, dtype=jnp.int32)
    own_pages = cast_rows.reshape(pages_own, 128)
    spread_slots = -(-pages_own // islands)
    deliver_slots = -(-capacity // islands)
    spread_ids = jnp.arange(spread_slots, dtype=jnp.int32)
    offset = jnp.mod(targets - my_index * pages_own, islands)
    local_index = offset[:, None] + islands * spread_ids[None, :]
    live_slot = (local_index < pages_own).reshape(-1, 1)
    outgoing = jnp.take(own_pages, jnp.clip(local_index, 0, pages_own - 1).reshape(-1), axis=0)
    outgoing = jnp.where(live_slot, outgoing, jnp.zeros_like(outgoing))
    spread = lax.all_to_all(outgoing, ISLAND, split_axis=0, concat_axis=0, tiled=True)
    deliver_ids = jnp.arange(deliver_slots, dtype=jnp.int32)
    first_page = range_start + jnp.mod(my_index - range_start, islands)
    global_page = first_page[:, None] + islands * deliver_ids[None, :]
    live_out = (global_page < (range_start + range_length)[:, None]).reshape(-1, 1)
    held_index = (
        global_page // pages_own * spread_slots + jnp.mod(global_page, pages_own) // islands
    )
    held_index = jnp.clip(held_index, 0, islands * spread_slots - 1).reshape(-1)
    forward = jnp.take(spread, held_index, axis=0)
    forward = jnp.where(live_out, forward, jnp.zeros_like(forward))
    delivered = lax.all_to_all(forward, ISLAND, split_axis=0, concat_axis=0, tiled=True)
    source = jnp.mod(own_start + slot_ids, islands) * deliver_slots + slot_ids // islands
    source = jnp.clip(source, 0, islands * deliver_slots - 1)
    packed = jnp.take(delivered, source, axis=0)
    packed = jnp.where((slot_ids < own_length)[:, None], packed, jnp.zeros_like(packed))
    return (new_master, new_momentum, packed[None])


def solution(mesh):
    split = Mesh(
        mesh.devices.reshape(16, 4, 4, 2), ("island_0", "island_1", "tensor_0", "tensor_1")
    )
    return jax.shard_map(
        body,
        mesh=split,
        in_specs=(P(ISLAND, None, TENSOR), P(ISLAND, TENSOR), P(ISLAND, TENSOR), P(), P()),
        out_specs=(P(ISLAND, TENSOR), P(ISLAND, TENSOR), P(ISLAND, None, TENSOR)),
        check_vma=False,
    )
```

profile of v0, /device:TPU:1, one launch (start us, length us, event | category | flops | bytes accessed | tf_op | source)
XLA Modules:
  0.0 187.8 jit_solution(3097106205375807306)
XLA Ops:
  0.6 3.9 %reshape_reshape_squeeze.3 = f32[16,4,2,6656]{3,2,1,0:T(2,128)S(1)} reshape(f32[1,128,6656]{2,1,0:T(8,128)} %param.5) | data formatting | bytes 6815744 | tf_op jit(solution)/shard_map/reshape;reshape;squeeze | solution.py:18
  4.6 0.2 copy.20
  4.8 40.6 %all_to_all.40 = f32[4,16,2,6656]{3,2,1,0:T(2,128)S(1)} all-to-all(f32[4,16,2,6656]{3,2,1,0:T(2,128)S(1)} %copy.20), channel_id=1, replica_groups=mesh['island_0'=16,'island_1'=4,'tensor_0'=4,'tensor_1'=2] {'island_1'}, dimensions={0} | all-to-all | bytes 6815744 | tf_op jit(solution)/shard_map/all_to_all | solution.py:23
  45.5 3.0 %reduce_sum.81 = f32[16,2,6656]{2,1,0:T(2,128)} reduce(f32[4,16,2,6656]{3,2,1,0:T(2,128)S(1)} %all_to_all.40, f32[]{:T(128)} %constant.132.clone.1), dimensions={0}, to_apply=%region_0.0 | reduce | flops 638976 | bytes 4259844 | tf_op jit(solution)/shard_map/reduce_sum | solution.py:24
  48.4 18.6 %all-to-all-start.1 = ((f32[16,2,6656]{2,1,0:T(2,128)}), f32[16,2,6656]{2,1,0:T(2,128)S(1)}, u32[]{:S(2)}, u32[]{:S(2)}) async-start(f32[16,2,6656]{2,1,0:T(2,128)} %reduce_sum.81), calls=%async_computation.1 | async-start | bytes 1703936 | tf_op jit(solution)/shard_map/all_to_all | solution.py:30
  67.2 0.1 min.40
  67.9 0.7 fusion.16
  68.7 35.8 %all-to-all-done.1 = f32[16,2,6656]{2,1,0:T(2,128)S(1)} async-done(((f32[16,2,6656]{2,1,0:T(2,128)}), f32[16,2,6656]{2,1,0:T(2,128)S(1)}, u32[]{:S(2)}, u32[]{:S(2)}) %all-to-all-start.1) | async-done | bytes 852000 | tf_op jit(solution)/shard_map/all_to_all | solution.py:30
  104.5 0.3 reduce_sum.82
  104.8 0.7 multiply_reduce_fusion
  105.5 0.6 broadcast_in_dim.109
  106.1 13.0 %all_to_all.41 = f32[8,1,1]{2,1,0:T(1,128)S(1)} all-to-all(f32[8,1,1]{2,1,0:T(1,128)S(1)} %broadcast_in_dim.109), channel_id=1, replica_groups=mesh['island_0'=16,'island_1'=4,'tensor_0'=4,'tensor_1'=2] {'tensor_0','..., dimensions={0} | all-to-all | bytes 64 | tf_op jit(solution)/shard_map/all_to_all | solution.py:35
  119.1 0.6 reduce_sum.84
  119.8 1.3 broadcast_in_dim.110
  121.0 9.7 %all-to-all-start.3 = ((f32[64,1,1]{2,1,0:T(1,128)}), f32[64,1,1]{2,1,0:T(1,128)S(1)}, u32[]{:S(2)}, u32[]{:S(2)}) async-start(f32[64,1,1]{2,1,0:T(1,128)} %broadcast_in_dim.110), calls=%async_computation.3 | async-start | bytes 65536 | tf_op jit(solution)/shard_map/all_to_all | solution.py:35
  130.8 0.1 copy.27
  131.5 0.1 ne.204
  131.6 12.5 %all-to-all-done.3 = f32[64,1,1]{2,1,0:T(1,128)S(1)} async-done(((f32[64,1,1]{2,1,0:T(1,128)}), f32[64,1,1]{2,1,0:T(1,128)S(1)}, u32[]{:S(2)}, u32[]{:S(2)}) %all-to-all-start.3) | async-done | bytes 288 | tf_op jit(solution)/shard_map/all_to_all | solution.py:35
  144.1 0.7 reduce_sum.85
  145.5 0.7 fusion.22
  146.3 0.7 gather_fusion
  147.0 0.8 broadcast_select_fusion.1
  147.8 4.6 %all-to-all-start.4 = ((bf16[64,2,128]{2,1,0:T(2,128)(2,1)}), bf16[64,2,128]{2,1,0:T(2,128)(2,1)S(1)}, u32[]{:S(2)}, u32[]{:S(2)}) async-start(bf16[64,2,128]{2,1,0:T(2,128)(2,1)} %broadcast_select_fusion.1), calls=%async_computation.4 | async-start | bytes 65536 | tf_op jit(solution)/shard_map/all_to_all | solution.py:87
  152.7 13.2 %all-to-all-done.4 = bf16[64,2,128]{2,1,0:T(2,128)(2,1)S(1)} async-done(((bf16[64,2,128]{2,1,0:T(2,128)(2,1)}), bf16[64,2,128]{2,1,0:T(2,128)(2,1)S(1)}, u32[]{:S(2)}, u32[]{:S(2)}) %all-to-all-start.4) | async-done | bytes 32800 | tf_op jit(solution)/shard_map/all_to_all | solution.py:87
  165.9 0.9 gather_fusion.1
  166.7 0.8 select_select_fusion
  167.6 4.6 %all-to-all-start.5 = ((bf16[64,4,128]{2,1,0:T(4,128)(2,1)}), bf16[64,4,128]{2,1,0:T(4,128)(2,1)S(1)}, u32[]{:S(2)}, u32[]{:S(2)}) async-start(bf16[64,4,128]{2,1,0:T(4,128)(2,1)} %select_select_fusion), calls=%async_computation.5 | async-start | bytes 131072 | tf_op jit(solution)/shard_map/all_to_all | solution.py:98
  172.2 0.6 compare_select_fusion
  172.8 1.3 compare_and_fusion.2
  174.1 12.1 %all-to-all-done.5 = bf16[64,4,128]{2,1,0:T(4,128)(2,1)S(1)} async-done(((bf16[64,4,128]{2,1,0:T(4,128)(2,1)}), bf16[64,4,128]{2,1,0:T(4,128)(2,1)S(1)}, u32[]{:S(2)}, u32[]{:S(2)}) %all-to-all-start.5) | async-done | bytes 65568 | tf_op jit(solution)/shard_map/all_to_all | solution.py:98
  186.2 0.8 gather_fusion.2
  187.0 0.7 fusion
  (35 shorter events, 1.8 us)
Async XLA Ops:
  45.4 21.9 %copy-start.2 = (s32[64]{0:T(128)S(1)}, s32[64]{0:T(128)}, u32[]{:S(2)}) copy-start(s32[64]{0:T(128)} %param.8) | copy-start | bytes 772
  45.4 22.2 %copy-start.3 = (s32[64]{0:T(128)S(1)}, s32[64]{0:T(128)}, u32[]{:S(2)}) copy-start(s32[64]{0:T(128)} %param.9) | copy-start | bytes 772
  45.4 100.1 %copy-start = (f32[2,6656]{1,0:T(2,128)S(1)}, f32[2,6656]{1,0:T(2,128)}, u32[]{:S(2)}) copy-start(f32[2,6656]{1,0:T(2,128)} %param.6) | copy-start | bytes 159748
  45.4 100.1 %copy-start.1 = (f32[2,6656]{1,0:T(2,128)S(1)}, f32[2,6656]{1,0:T(2,128)}, u32[]{:S(2)}) copy-start(f32[2,6656]{1,0:T(2,128)} %param.7) | copy-start | bytes 159748
  48.4 56.1 %all-to-all-start.1 = ((f32[16,2,6656]{2,1,0:T(2,128)}), f32[16,2,6656]{2,1,0:T(2,128)S(1)}, u32[]{:S(2)}, u32[]{:S(2)}) async-start(f32[16,2,6656]{2,1,0:T(2,128)} %reduce_sum.81), calls=%async_computation.1 | async-start | bytes 1703936 | tf_op jit(solution)/shard_map/all_to_all | solution.py:30
  121.0 23.1 %all-to-all-start.3 = ((f32[64,1,1]{2,1,0:T(1,128)}), f32[64,1,1]{2,1,0:T(1,128)S(1)}, u32[]{:S(2)}, u32[]{:S(2)}) async-start(f32[64,1,1]{2,1,0:T(1,128)} %broadcast_in_dim.110), calls=%async_computation.3 | async-start | bytes 65536 | tf_op jit(solution)/shard_map/all_to_all | solution.py:35
  147.8 18.1 %all-to-all-start.4 = ((bf16[64,2,128]{2,1,0:T(2,128)(2,1)}), bf16[64,2,128]{2,1,0:T(2,128)(2,1)S(1)}, u32[]{:S(2)}, u32[]{:S(2)}) async-start(bf16[64,2,128]{2,1,0:T(2,128)(2,1)} %broadcast_select_fusion.1), calls=%async_computation.4 | async-start | bytes 65536 | tf_op jit(solution)/shard_map/all_to_all | solution.py:87
  167.6 18.6 %all-to-all-start.5 = ((bf16[64,4,128]{2,1,0:T(4,128)(2,1)}), bf16[64,4,128]{2,1,0:T(4,128)(2,1)S(1)}, u32[]{:S(2)}, u32[]{:S(2)}) async-start(bf16[64,4,128]{2,1,0:T(4,128)(2,1)} %select_select_fusion), calls=%async_computation.5 | async-start | bytes 131072 | tf_op jit(solution)/shard_map/all_to_all | solution.py:98
where the time goes:
time: 190 us; the launch traced here: 188 us
  waiting for transfers between devices  73.6 us (39%)
  blocking collectives  53.6 us (28%)
  starting transfers between devices  37.5 us (20%)
  other arithmetic  11.6 us (6%)
  local copies, waits for them, and re-layouts  9.92 us (5%)
    all_to_all x1, blocking collectives, sent_and_summed(): lax.all_to_all(tiles, axis, split_axis=0, concat_axis=0, tiled=True)  40.6 us
    all_to_all x1, waiting for transfers between devices, sum_in_two_steps(): return jnp.sum(lax.all_to_all(own, far, 0, 0, tiled=True), axis=0)  35.8 us
    all_to_all x1, starting transfers between devices, sum_in_two_steps(): return jnp.sum(lax.all_to_all(own, far, 0, 0, tiled=True), axis=0)  18.6 us
    all_to_all x1, waiting for transfers between devices, body(): lax.all_to_all(outgoing, ISLAND, split_axis=0, concat_axis=0, tiled=True)  13.2 us
    all_to_all x1, blocking collectives, copy_for_each(): lax.all_to_all(jnp.broadcast_to(array[None], (length, *array.shape)), axi...  13 us
    all_to_all x1, waiting for transfers between devices, copy_for_each(): lax.all_to_all(jnp.broadcast_to(array[None], (length, *array.shape)), axi...  12.5 us
    all_to_all x1, waiting for transfers between devices, body(): lax.all_to_all(forward, ISLAND, split_axis=0, concat_axis=0, tiled=True)  12.1 us
    all_to_all x1, starting transfers between devices, copy_for_each(): lax.all_to_all(jnp.broadcast_to(array[None], (length, *array.shape)), axi...  9.71 us
  transfers between devices with their start and end apart: 4, of which 4 were waited for; matrix products, arithmetic and copies ran while one was open for 3% of the time, Pallas kernels for 0%

commit v1 on v0

v1 whole, which is shorter than its diff:
```python
import jax
import jax.numpy as jnp
from jax import lax
from jax.sharding import Mesh
from jax.sharding import PartitionSpec as P

ISLAND = ("z", "y")
TENSOR = ("x", "core")

epsilon = 1e-06
decay_rate = 0.9
outer_rate = 0.7

NZ, NY, ROW_TILES, GROUPS, LANES = 16, 4, 16, 13, 128
PER_ROW = NY * GROUPS


def shift(n, by):
    return [(i, (i + by) % n) for i in range(n)]


def pick(array, index, axis_size):
    return lax.dynamic_index_in_dim(array, index % axis_size, 0, keepdims=False)


def summed_around(classes, axis, n):
    here = lax.axis_index(axis)
    half = classes.shape[1] // 2
    up, down = shift(n, 1), shift(n, -1)
    far = pick(classes, here + 2, 4)
    passed_up = lax.ppermute(far[:half], axis, up)
    passed_down = lax.ppermute(far[half:], axis, down)
    above, below, own = pick(classes, here + 1, 4), pick(classes, here + 3, 4), pick(classes, here, 4)
    near_up = lax.ppermute(above[half:], axis, up)
    near_down = lax.ppermute(below[:half], axis, down)
    joined_up = lax.ppermute(above[:half] + passed_up, axis, up)
    joined_down = lax.ppermute(below[half:] + passed_down, axis, down)
    return jnp.concatenate([own[:half] + near_down + joined_up, own[half:] + near_up + joined_down], axis=0)


def exchanged(array, axes):
    return lax.all_to_all(array, axes, 0, 0, tiled=True)


def rows_of(array, index):
    return array.at[index].get(mode="promise_in_bounds")


def body(pseudo_grad, outer_params, momentum, save_pages, writer):
    z, y = lax.axis_index("z"), lax.axis_index("y")
    islands = NZ * NY
    entries = pseudo_grad.shape[1] * pseudo_grad.shape[2] * lax.axis_size(TENSOR)

    starts = jnp.cumsum(save_pages) - save_pages
    targets = jnp.arange(islands, dtype=jnp.int32)
    owner_table = writer[None, :] == targets[:, None]
    range_start = jnp.sum(jnp.where(owner_table, starts[None, :], 0), axis=1)
    range_length = jnp.sum(jnp.where(owner_table, save_pages[None, :], 0), axis=1)
    slots = jnp.arange(4, dtype=jnp.int32)
    first_row = (range_start // PER_ROW)[:, None]
    near_row = first_row + (slots[None, :] - first_row) % 4
    held_index = jnp.zeros((islands, 4), jnp.int32)
    sum_index = jnp.zeros((islands, 4), jnp.int32)
    for row in (near_row, near_row + 4):
        tile_row = row // 8
        group = (z - GROUPS * tile_row) % NZ
        page = PER_ROW * row + NY * group + y
        inside = (group < GROUPS) & (page >= range_start[:, None]) & (page < (range_start + range_length)[:, None])
        held_index = jnp.where(inside, row, held_index)
        sum_index = jnp.where(inside, 8 * ((GROUPS * tile_row + group) // NZ) + row % 8, sum_index)
    target_z, target_y = targets // NY, targets % NY
    group = (z - GROUPS * target_z) % NZ
    row_tile = jnp.where(group < GROUPS, (GROUPS * target_z + group) // NZ, 0)
    row_index = (8 * row_tile + 2 * target_y)[:, None] + jnp.arange(2, dtype=jnp.int32)[None, :]
    send_index = jnp.concatenate([sum_index, row_index, jnp.zeros((islands, 2), jnp.int32)], axis=1).reshape(-1)
    is_mine = targets == z * NY + y
    own_start = jnp.sum(jnp.where(is_mine, range_start, 0))
    own_length = jnp.sum(jnp.where(is_mine, range_length, 0))
    place = jnp.arange(208, dtype=jnp.int32)
    page = jnp.minimum(own_start + place, 6655)
    row, block = page // PER_ROW, page % PER_ROW
    source = ((GROUPS * (row // 8) + block // NY) % NZ) * NY + block % NY
    slot = row % 4

    settled = outer_params - (outer_rate * decay_rate * decay_rate) * momentum
    settled = settled.reshape(2, GROUPS, NY, LANES).transpose(1, 2, 0, 3)
    settled = jnp.concatenate([settled, jnp.zeros((NZ - GROUPS, NY, 2, LANES), jnp.float32)], axis=0)
    settled = jnp.concatenate([settled, settled], axis=0)
    spread = lax.dynamic_slice_in_dim(settled, (-GROUPS * z) % NZ, NZ, 0)
    held = exchanged(spread.reshape(islands, 2, LANES), ISLAND).reshape(-1, LANES)
    settled_out = rows_of(held, held_index.reshape(-1)).reshape(islands, 4, LANES)
    settled_in = exchanged(settled_out, ISLAND).reshape(-1, LANES)
    settled_pages = rows_of(settled_in, source * 4 + slot)

    tiles = pseudo_grad[0].reshape(ROW_TILES, 8, GROUPS, NY, LANES).transpose(3, 0, 2, 1, 4)
    over_y = summed_around(tiles.reshape(NY, ROW_TILES * GROUPS, 8, LANES), "y", NY)
    classes = over_y.reshape(GROUPS, 4, 4, 8, LANES).transpose(2, 1, 0, 3, 4)
    windows = summed_around(classes.reshape(4, 4 * GROUPS, 8, LANES), "z", NZ).reshape(4, GROUPS, 8, LANES)
    far = [[4 * h + l for h in range(4)] for l in range(4)]
    summed = lax.all_to_all(windows, "z", 0, 0, tiled=True, axis_index_groups=far).sum(axis=0)
    outer_grad = summed / islands
    part = jnp.sum(outer_grad * outer_grad)

    outgoing = rows_of(outer_grad.reshape(-1, LANES), send_index).reshape(islands, 8, LANES)
    outgoing = jnp.where(jnp.arange(8)[None, :, None] < 6, outgoing, part)
    arrived = exchanged(outgoing, ISLAND)
    over_islands = jnp.sum(arrived[:, 6, 0])
    eight = exchanged(jnp.broadcast_to(over_islands, (lax.axis_size(TENSOR), 1, 1)), TENSOR)
    square_sum = jnp.sum(eight)
    scale = 1.0 / jnp.sqrt(square_sum / entries + epsilon)

    mine = arrived[:, 4:6].reshape(NZ, NY, 2, LANES)
    mine = lax.dynamic_slice_in_dim(jnp.concatenate([mine, mine], axis=0), (GROUPS * z) % NZ, GROUPS, 0)
    normed = mine.transpose(2, 0, 1, 3).reshape(2, -1) * scale
    new_momentum = decay_rate * momentum + normed
    new_master = outer_params - outer_rate * (normed + decay_rate * new_momentum)
    gradient_pages = rows_of(arrived.reshape(-1, LANES), source * 8 + slot)
    pages = settled_pages - (outer_rate * (1.0 + decay_rate)) * (gradient_pages * scale)
    packed = jnp.where((place < own_length)[:, None], pages, 0.0).astype(jnp.bfloat16)
    return (new_master, new_momentum, packed[None])


def solution(mesh):
    split = Mesh(mesh.devices.reshape(NZ, NY, 4, 2), ("z", "y", "x", "core"))
    return jax.shard_map(
        body,
        mesh=split,
        in_specs=(P(ISLAND, None, TENSOR), P(ISLAND, TENSOR), P(ISLAND, TENSOR), P(), P()),
        out_specs=(P(ISLAND, TENSOR), P(ISLAND, TENSOR), P(ISLAND, None, TENSOR)),
        check_vma=False,
    )
```

time: 190 us -> 191 us (level)
  starting transfers between devices: 37.5 us -> 73.2 us
  blocking collectives: 53.6 us -> 19.5 us
  waiting for transfers between devices: 73.6 us -> 70.7 us
  other arithmetic: 11.6 us -> 13.6 us
    ppermute x0 -> x12, starting transfers between devices: none -> 49.8 us  [the longest x2 12.9 us: summed_around(): passed_down = lax.ppermute(far[half:], axis, down)]
    all_to_all x2 -> x1, blocking collectives: 53.6 us -> 19.5 us  [exchanged(): return lax.all_to_all(array, axes, 0, 0, tiled=True)]
    all_to_all x4, waiting for transfers between devices: 73.6 us -> 56.1 us  [the longest x3 43.8 us: exchanged(): return lax.all_to_all(array, axes, 0, 0, tiled=True)]
    ppermute x0 -> x12, waiting for transfers between devices: none -> 14.6 us  [the longest x2 7.59 us: summed_around(): joined_down = lax.ppermute(below[half:] + passed_down, axis, down)]
    all_to_all x4, starting transfers between devices: 37.5 us -> 23.3 us  [the longest x3 16.2 us: exchanged(): return lax.all_to_all(array, axes, 0, 0, tiled=True)]
    add x0 -> x8, other arithmetic: none -> 4.43 us  [the longest x2 2.33 us: summed_around(): own[:half] + near_down + joined_up]
    reduce_sum x5 -> x4, other arithmetic: 5.17 us -> 1.9 us  [the longest x1 0.67 us: body(): over_islands = jnp.sum(arrived[:, 6, 0])]
    concatenate x0 -> x4, other arithmetic: none -> 1.95 us  [the longest x2 1.76 us: summed_around(): jnp.concatenate([own[:half] + near_down + joined_up, own[half:] + near_up...]
  transfers between devices with their start and end apart: 4 -> 16, of which waited for: 4 -> 10; matrix products, arithmetic and copies ran while one was open for 3% -> 4% of each run, Pallas kernels for 0% -> 0%
where the time goes in v1:
time: 191 us; the launch traced here: 189 us
  starting transfers between devices  73.2 us (38%)
  waiting for transfers between devices  70.7 us (37%)
  blocking collectives  19.5 us (10%)
  other arithmetic  13.6 us (7%)
  local copies, waits for them, and re-layouts  9.66 us (5%)
  between operations  1.96 us (1%)
    all_to_all x3, waiting for transfers between devices, exchanged(): return lax.all_to_all(array, axes, 0, 0, tiled=True)  43.8 us
    all_to_all x1, blocking collectives, exchanged(): return lax.all_to_all(array, axes, 0, 0, tiled=True)  19.5 us
    all_to_all x3, starting transfers between devices, exchanged(): return lax.all_to_all(array, axes, 0, 0, tiled=True)  16.2 us
    ppermute x2, starting transfers between devices, summed_around(): passed_down = lax.ppermute(far[half:], axis, down)  12.9 us
    all_to_all x1, waiting for transfers between devices, body(): lax.all_to_all(windows, 'z', 0, 0, tiled=True, axis_index_groups=far)  12.3 us
    ppermute x2, starting transfers between devices, summed_around(): passed_up = lax.ppermute(far[:half], axis, up)  9.38 us
    ppermute x2, starting transfers between devices, summed_around(): joined_down = lax.ppermute(below[half:] + passed_down, axis, down)  8.05 us
    ppermute x2, waiting for transfers between devices, summed_around(): joined_down = lax.ppermute(below[half:] + passed_down, axis, down)  7.59 us
  transfers between devices with their start and end apart: 16, of which 10 were waited for; matrix products, arithmetic and copies ran while one was open for 4% of the time, Pallas kernels for 0%

profile of v1, /device:TPU:1, one launch (start us, length us, event | category | flops | bytes accessed | tf_op | source)
XLA Modules:
  0.0 188.6 jit_solution(8434607477819071383)
XLA Ops:
  0.7 2.2 %copy.50 = f32[16,8,13,4,128]{4,1,2,0,3:T(8,128)S(1)} copy(f32[16,8,13,4,128]{4,1,3,2,0:T(8,128)} %bitcast.94) | data formatting | bytes 6815744 | tf_op jit(solution)/shard_map/reshape;squeeze | solution.py:95
  2.9 1.1 dynamic-slice_bitcast_fusion.6
  4.0 4.0 %collective-permute-start.1 = (f32[104,8,128]{2,1,0:T(8,128)S(1)}, f32[104,8,128]{2,1,0:T(8,128)S(1)}, u32[]{:S(2)}, u32[]{:S(2)}) collective-permute-start(f32[104,8,128]{2,1,0:T(8,128)S(1)} %get-tuple-element.10), channel_id=1, source_target_pairs={{0,8},{8,16},{16,24},{24,0},{1,9},{9,17},{17,25},{25,1},{2,10},{10... | collective-permute-start | bytes 1277960 | tf_op jit(solution)/shard_map/ppermute | solution.py:31
  8.0 3.4 %collective-permute-start = (f32[104,8,128]{2,1,0:T(8,128)}, f32[104,8,128]{2,1,0:T(8,128)}, u32[]{:S(2)}, u32[]{:S(2)}) collective-permute-start(f32[104,8,128]{2,1,0:T(8,128)} %get-tuple-element.9), channel_id=1, source_target_pairs={{0,24},{8,0},{16,8},{24,16},{1,25},{9,1},{17,9},{25,17},{2,26},{10... | collective-permute-start | bytes 1277960 | tf_op jit(solution)/shard_map/ppermute | solution.py:35
  11.4 3.4 %collective-permute-start.4 = (f32[104,8,128]{2,1,0:T(8,128)}, f32[104,8,128]{2,1,0:T(8,128)}, u32[]{:S(2)}, u32[]{:S(2)}) collective-permute-start(f32[104,8,128]{2,1,0:T(8,128)} %get-tuple-element.11), channel_id=1, source_target_pairs={{0,24},{8,0},{16,8},{24,16},{1,25},{9,1},{17,9},{25,17},{2,26},{10... | collective-permute-start | bytes 1277960 | tf_op jit(solution)/shard_map/ppermute | solution.py:32
  15.8 4.7 %collective-permute-start.2 = (f32[104,8,128]{2,1,0:T(8,128)}, f32[104,8,128]{2,1,0:T(8,128)}, u32[]{:S(2)}, u32[]{:S(2)}) collective-permute-start(f32[104,8,128]{2,1,0:T(8,128)} %fusion.3), channel_id=1, source_target_pairs={{0,8},{8,16},{16,24},{24,0},{1,9},{9,17},{17,25},{25,1},{2,10},{10... | collective-permute-start | bytes 1277960 | tf_op jit(solution)/shard_map/ppermute | solution.py:36
  20.5 4.1 %collective-permute-start.3 = (f32[104,8,128]{2,1,0:T(8,128)}, f32[104,8,128]{2,1,0:T(8,128)}, u32[]{:S(2)}, u32[]{:S(2)}) collective-permute-start(f32[104,8,128]{2,1,0:T(8,128)} %get-tuple-element.12), channel_id=1, source_target_pairs={{0,8},{8,16},{16,24},{24,0},{1,9},{9,17},{17,25},{25,1},{2,10},{10... | collective-permute-start | bytes 1277960 | tf_op jit(solution)/shard_map/ppermute | solution.py:34
  24.7 1.2 collective-permute-done.4
  25.9 2.8 %collective-permute-done.2 = f32[104,8,128]{2,1,0:T(8,128)} collective-permute-done((f32[104,8,128]{2,1,0:T(8,128)}, f32[104,8,128]{2,1,0:T(8,128)}, u32[]{:S(2)}, u32[]{:S(2)}) %collective-permute-start.2) | collective-permute-done | bytes 426016 | tf_op jit(solution)/shard_map/ppermute | solution.py:36
  28.7 2.3 %fusion.5 = (f32[104,8,128]{2,1,0:T(8,128)}, f32[104,8,128]{2,1,0:T(8,128)}) fusion(f32[104,8,128]{2,1,0:T(8,128)} %collective-permute-done.2, f32[104,8,128]{2,1,0:T(8,128)} %collective-permute-done, f32[4,208,8,128]{3,2,1,0:T(8,128)S(1)} %bitcast.90, s32[]{:T(128)S(6)} %select_n.415, f32[104,8,128]{2,1,0:T(8,128)} %collective-permute-done.4, ...), kind=kLoop, calls=%fused_computation.18 | loop fusion | flops 319488 | bytes 2981900 | tf_op jit(solution)/shard_map/add | solution.py:38
  31.0 6.1 %collective-permute-start.5 = (f32[104,8,128]{2,1,0:T(8,128)}, f32[104,8,128]{2,1,0:T(8,128)}, u32[]{:S(2)}, u32[]{:S(2)}) collective-permute-start(f32[104,8,128]{2,1,0:T(8,128)} %get-tuple-element.8), channel_id=1, source_target_pairs={{0,24},{8,0},{16,8},{24,16},{1,25},{9,1},{17,9},{25,17},{2,26},{10... | collective-permute-start | bytes 1277960 | tf_op jit(solution)/shard_map/ppermute | solution.py:37
  38.3 4.2 %collective-permute-done.5 = f32[104,8,128]{2,1,0:T(8,128)} collective-permute-done((f32[104,8,128]{2,1,0:T(8,128)}, f32[104,8,128]{2,1,0:T(8,128)}, u32[]{:S(2)}, u32[]{:S(2)}) %collective-permute-start.5) | collective-permute-done | bytes 426016 | tf_op jit(solution)/shard_map/ppermute | solution.py:37
  42.5 1.2 fusion.2
  44.9 5.4 %collective-permute-start.7 = (f32[26,8,128]{2,1,0:T(8,128)S(1)}, f32[26,8,128]{2,1,0:T(8,128)S(1)}, u32[]{:S(2)}, u32[]{:S(2)}) collective-permute-start(f32[26,8,128]{2,1,0:T(8,128)S(1)} %get-tuple-element.16), channel_id=1, source_target_pairs={{0,32},{32,64},{64,96},{96,128},{128,160},{160,192},{192,224},{224... | collective-permute-start | bytes 319496 | tf_op jit(solution)/shard_map/ppermute | solution.py:31
  50.3 9.5 %collective-permute-start.10 = (f32[26,8,128]{2,1,0:T(8,128)S(1)}, f32[26,8,128]{2,1,0:T(8,128)S(1)}, u32[]{:S(2)}, u32[]{:S(2)}) collective-permute-start(f32[26,8,128]{2,1,0:T(8,128)S(1)} %get-tuple-element.17), channel_id=1, source_target_pairs={{0,480},{32,0},{64,32},{96,64},{128,96},{160,128},{192,160},{224,1... | collective-permute-start | bytes 319496 | tf_op jit(solution)/shard_map/ppermute | solution.py:32
  59.8 3.4 %collective-permute-start.6 = (f32[26,8,128]{2,1,0:T(8,128)S(1)}, f32[26,8,128]{2,1,0:T(8,128)S(1)}, u32[]{:S(2)}, u32[]{:S(2)}) collective-permute-start(f32[26,8,128]{2,1,0:T(8,128)S(1)} %get-tuple-element.15), channel_id=1, source_target_pairs={{0,480},{32,0},{64,32},{96,64},{128,96},{160,128},{192,160},{224,1... | collective-permute-start | bytes 319496 | tf_op jit(solution)/shard_map/ppermute | solution.py:35
  63.2 2.1 %collective-permute-start.8 = (f32[26,8,128]{2,1,0:T(8,128)S(1)}, f32[26,8,128]{2,1,0:T(8,128)S(1)}, u32[]{:S(2)}, u32[]{:S(2)}) collective-permute-start(f32[26,8,128]{2,1,0:T(8,128)S(1)} %fusion.9), channel_id=1, source_target_pairs={{0,32},{32,64},{64,96},{96,128},{128,160},{160,192},{192,224},{224... | collective-permute-start | bytes 319496 | tf_op jit(solution)/shard_map/ppermute | solution.py:36
  65.3 1.9 %collective-permute-start.9 = (f32[26,8,128]{2,1,0:T(8,128)S(1)}, f32[26,8,128]{2,1,0:T(8,128)S(1)}, u32[]{:S(2)}, u32[]{:S(2)}) collective-permute-start(f32[26,8,128]{2,1,0:T(8,128)S(1)} %get-tuple-element.18), channel_id=1, source_target_pairs={{0,32},{32,64},{64,96},{96,128},{128,160},{160,192},{192,224},{224... | collective-permute-start | bytes 319496 | tf_op jit(solution)/shard_map/ppermute | solution.py:34
  67.3 2.8 %collective-permute-done.8 = f32[26,8,128]{2,1,0:T(8,128)S(1)} collective-permute-done((f32[26,8,128]{2,1,0:T(8,128)S(1)}, f32[26,8,128]{2,1,0:T(8,128)S(1)}, u32[]{:S(2)}, u32[]{:S(2)}) %collective-permute-start.8) | collective-permute-done | bytes 106528 | tf_op jit(solution)/shard_map/ppermute | solution.py:36
  70.1 1.9 %collective-permute-start.11 = (f32[26,8,128]{2,1,0:T(8,128)S(1)}, f32[26,8,128]{2,1,0:T(8,128)S(1)}, u32[]{:S(2)}, u32[]{:S(2)}) collective-permute-start(f32[26,8,128]{2,1,0:T(8,128)S(1)} %get-tuple-element.14), channel_id=1, source_target_pairs={{0,480},{32,0},{64,32},{96,64},{128,96},{160,128},{192,160},{224,1... | collective-permute-start | bytes 319496 | tf_op jit(solution)/shard_map/ppermute | solution.py:37
  72.1 3.4 %collective-permute-done.11 = f32[26,8,128]{2,1,0:T(8,128)S(1)} collective-permute-done((f32[26,8,128]{2,1,0:T(8,128)S(1)}, f32[26,8,128]{2,1,0:T(8,128)S(1)}, u32[]{:S(2)}, u32[]{:S(2)}) %collective-permute-start.11) | collective-permute-done | bytes 106528 | tf_op jit(solution)/shard_map/ppermute | solution.py:37
  76.2 7.1 %all-to-all-start = ((f32[4,13,8,128]{3,2,1,0:T(8,128)}), f32[4,13,8,128]{3,2,1,0:T(8,128)S(1)}, u32[]{:S(2)}, u32[]{:S(2)}) async-start(f32[4,13,8,128]{3,2,1,0:T(8,128)} %bitcast.23), calls=%async_computation | async-start | bytes 425984 | tf_op jit(solution)/shard_map/all_to_all | solution.py:100
  83.6 12.3 %all-to-all-done = f32[4,13,8,128]{3,2,1,0:T(8,128)S(1)} async-done(((f32[4,13,8,128]{3,2,1,0:T(8,128)}), f32[4,13,8,128]{3,2,1,0:T(8,128)S(1)}, u32[]{:S(2)}, u32[]{:S(2)}) %all-to-all-start) | async-done | bytes 213024 | tf_op jit(solution)/shard_map/all_to_all | solution.py:100
  97.6 1.4 bitcast_select_fusion
  99.0 7.0 %all-to-all-start.1 = ((f32[64,8,128]{2,1,0:T(8,128)}), f32[64,8,128]{2,1,0:T(8,128)S(1)}, u32[]{:S(2)}, u32[]{:S(2)}) async-start(f32[64,8,128]{2,1,0:T(8,128)} %bitcast_select_fusion), calls=%async_computation.1 | async-start | bytes 524288 | tf_op jit(solution)/shard_map/all_to_all | solution.py:42
  106.7 16.9 %all-to-all-done.1 = f32[64,8,128]{2,1,0:T(8,128)S(1)} async-done(((f32[64,8,128]{2,1,0:T(8,128)}), f32[64,8,128]{2,1,0:T(8,128)S(1)}, u32[]{:S(2)}, u32[]{:S(2)}) %all-to-all-start.1) | async-done | bytes 262176 | tf_op jit(solution)/shard_map/all_to_all | solution.py:42
  125.0 19.5 %all_to_all.25 = f32[8,1,1]{2,1,0:T(1,128)S(1)} all-to-all(f32[8,1,1]{2,1,0:T(1,128)S(1)} %broadcast_in_dim.80), channel_id=1, replica_groups=mesh['z'=16,'y'=4,'x'=4,'core'=2] {'x','core'}, dimensions={0} | all-to-all | bytes 64 | tf_op jit(solution)/shard_map/all_to_all | solution.py:42
  147.6 4.6 %all-to-all-start.3 = ((f32[64,2,128]{2,1,0:T(2,128)}), f32[64,2,128]{2,1,0:T(2,128)S(1)}, u32[]{:S(2)}, u32[]{:S(2)}) async-start(f32[64,2,128]{2,1,0:T(2,128)} %bitcast.31), calls=%async_computation.3 | async-start | bytes 131072 | tf_op jit(solution)/shard_map/all_to_all | solution.py:42
  152.2 13.9 %all-to-all-done.3 = f32[64,2,128]{2,1,0:T(2,128)S(1)} async-done(((f32[64,2,128]{2,1,0:T(2,128)}), f32[64,2,128]{2,1,0:T(2,128)S(1)}, u32[]{:S(2)}, u32[]{:S(2)}) %all-to-all-start.3) | async-done | bytes 65568 | tf_op jit(solution)/shard_map/all_to_all | solution.py:42
  166.1 1.3 gather_fusion.1
  167.5 4.7 %all-to-all-start.4 = ((f32[64,4,128]{2,1,0:T(4,128)}), f32[64,4,128]{2,1,0:T(4,128)S(1)}, u32[]{:S(2)}, u32[]{:S(2)}) async-start(f32[64,4,128]{2,1,0:T(4,128)} %bitcast.34), calls=%async_computation.4 | async-start | bytes 262144 | tf_op jit(solution)/shard_map/all_to_all | solution.py:42
  174.2 13.0 %all-to-all-done.4 = f32[64,4,128]{2,1,0:T(4,128)S(1)} async-done(((f32[64,4,128]{2,1,0:T(4,128)}), f32[64,4,128]{2,1,0:T(4,128)S(1)}, u32[]{:S(2)}, u32[]{:S(2)}) %all-to-all-start.4) | async-done | bytes 131104 | tf_op jit(solution)/shard_map/all_to_all | solution.py:42
  (72 shorter events, 14.0 us)
Async XLA Ops:
  2.9 34.3 %copy-start.2 = (s32[64]{0:T(128)S(1)}, s32[64]{0:T(128)}, u32[]{:S(2)}) copy-start(s32[64]{0:T(128)} %param.8) | copy-start | bytes 772
  2.9 34.6 %copy-start.3 = (s32[64]{0:T(128)S(1)}, s32[64]{0:T(128)}, u32[]{:S(2)}) copy-start(s32[64]{0:T(128)} %param.9) | copy-start | bytes 772
  4.0 11.0 %collective-permute-start.1 = (f32[104,8,128]{2,1,0:T(8,128)S(1)}, f32[104,8,128]{2,1,0:T(8,128)S(1)}, u32[]{:S(2)}, u32[]{:S(2)}) collective-permute-start(f32[104,8,128]{2,1,0:T(8,128)S(1)} %get-tuple-element.10), channel_id=1, source_target_pairs={{0,8},{8,16},{16,24},{24,0},{1,9},{9,17},{17,25},{25,1},{2,10},{10... | collective-permute-start | bytes 1277960 | tf_op jit(solution)/shard_map/ppermute | solution.py:31
  8.0 16.6 %collective-permute-start = (f32[104,8,128]{2,1,0:T(8,128)}, f32[104,8,128]{2,1,0:T(8,128)}, u32[]{:S(2)}, u32[]{:S(2)}) collective-permute-start(f32[104,8,128]{2,1,0:T(8,128)} %get-tuple-element.9), channel_id=1, source_target_pairs={{0,24},{8,0},{16,8},{24,16},{1,25},{9,1},{17,9},{25,17},{2,26},{10... | collective-permute-start | bytes 1277960 | tf_op jit(solution)/shard_map/ppermute | solution.py:35
  11.4 14.5 %collective-permute-start.4 = (f32[104,8,128]{2,1,0:T(8,128)}, f32[104,8,128]{2,1,0:T(8,128)}, u32[]{:S(2)}, u32[]{:S(2)}) collective-permute-start(f32[104,8,128]{2,1,0:T(8,128)} %get-tuple-element.11), channel_id=1, source_target_pairs={{0,24},{8,0},{16,8},{24,16},{1,25},{9,1},{17,9},{25,17},{2,26},{10... | collective-permute-start | bytes 1277960 | tf_op jit(solution)/shard_map/ppermute | solution.py:32
  15.8 12.9 %collective-permute-start.2 = (f32[104,8,128]{2,1,0:T(8,128)}, f32[104,8,128]{2,1,0:T(8,128)}, u32[]{:S(2)}, u32[]{:S(2)}) collective-permute-start(f32[104,8,128]{2,1,0:T(8,128)} %fusion.3), channel_id=1, source_target_pairs={{0,8},{8,16},{16,24},{24,0},{1,9},{9,17},{17,25},{25,1},{2,10},{10... | collective-permute-start | bytes 1277960 | tf_op jit(solution)/shard_map/ppermute | solution.py:36
  20.5 17.8 %collective-permute-start.3 = (f32[104,8,128]{2,1,0:T(8,128)}, f32[104,8,128]{2,1,0:T(8,128)}, u32[]{:S(2)}, u32[]{:S(2)}) collective-permute-start(f32[104,8,128]{2,1,0:T(8,128)} %get-tuple-element.12), channel_id=1, source_target_pairs={{0,8},{8,16},{16,24},{24,0},{1,9},{9,17},{17,25},{25,1},{2,10},{10... | collective-permute-start | bytes 1277960 | tf_op jit(solution)/shard_map/ppermute | solution.py:34
  31.0 11.5 %collective-permute-start.5 = (f32[104,8,128]{2,1,0:T(8,128)}, f32[104,8,128]{2,1,0:T(8,128)}, u32[]{:S(2)}, u32[]{:S(2)}) collective-permute-start(f32[104,8,128]{2,1,0:T(8,128)} %get-tuple-element.8), channel_id=1, source_target_pairs={{0,24},{8,0},{16,8},{24,16},{1,25},{9,1},{17,9},{25,17},{2,26},{10... | collective-permute-start | bytes 1277960 | tf_op jit(solution)/shard_map/ppermute | solution.py:37
  44.9 18.3 %collective-permute-start.7 = (f32[26,8,128]{2,1,0:T(8,128)S(1)}, f32[26,8,128]{2,1,0:T(8,128)S(1)}, u32[]{:S(2)}, u32[]{:S(2)}) collective-permute-start(f32[26,8,128]{2,1,0:T(8,128)S(1)} %get-tuple-element.16), channel_id=1, source_target_pairs={{0,32},{32,64},{64,96},{96,128},{128,160},{160,192},{192,224},{224... | collective-permute-start | bytes 319496 | tf_op jit(solution)/shard_map/ppermute | solution.py:31
  50.3 17.0 %collective-permute-start.10 = (f32[26,8,128]{2,1,0:T(8,128)S(1)}, f32[26,8,128]{2,1,0:T(8,128)S(1)}, u32[]{:S(2)}, u32[]{:S(2)}) collective-permute-start(f32[26,8,128]{2,1,0:T(8,128)S(1)} %get-tuple-element.17), channel_id=1, source_target_pairs={{0,480},{32,0},{64,32},{96,64},{128,96},{160,128},{192,160},{224,1... | collective-permute-start | bytes 319496 | tf_op jit(solution)/shard_map/ppermute | solution.py:32
  59.8 7.5 %collective-permute-start.6 = (f32[26,8,128]{2,1,0:T(8,128)S(1)}, f32[26,8,128]{2,1,0:T(8,128)S(1)}, u32[]{:S(2)}, u32[]{:S(2)}) collective-permute-start(f32[26,8,128]{2,1,0:T(8,128)S(1)} %get-tuple-element.15), channel_id=1, source_target_pairs={{0,480},{32,0},{64,32},{96,64},{128,96},{160,128},{192,160},{224,1... | collective-permute-start | bytes 319496 | tf_op jit(solution)/shard_map/ppermute | solution.py:35
  63.2 82.7 %copy-start = (f32[2,6656]{1,0:T(2,128)S(1)}, f32[2,6656]{1,0:T(2,128)}, u32[]{:S(2)}) copy-start(f32[2,6656]{1,0:T(2,128)} %param.6) | copy-start | bytes 159748
  63.2 82.7 %copy-start.1 = (f32[2,6656]{1,0:T(2,128)S(1)}, f32[2,6656]{1,0:T(2,128)}, u32[]{:S(2)}) copy-start(f32[2,6656]{1,0:T(2,128)} %param.7) | copy-start | bytes 159748
  63.2 6.8 %collective-permute-start.8 = (f32[26,8,128]{2,1,0:T(8,128)S(1)}, f32[26,8,128]{2,1,0:T(8,128)S(1)}, u32[]{:S(2)}, u32[]{:S(2)}) collective-permute-start(f32[26,8,128]{2,1,0:T(8,128)S(1)} %fusion.9), channel_id=1, source_target_pairs={{0,32},{32,64},{64,96},{96,128},{128,160},{160,192},{192,224},{224... | collective-permute-start | bytes 319496 | tf_op jit(solution)/shard_map/ppermute | solution.py:36
  65.3 6.8 %collective-permute-start.9 = (f32[26,8,128]{2,1,0:T(8,128)S(1)}, f32[26,8,128]{2,1,0:T(8,128)S(1)}, u32[]{:S(2)}, u32[]{:S(2)}) collective-permute-start(f32[26,8,128]{2,1,0:T(8,128)S(1)} %get-tuple-element.18), channel_id=1, source_target_pairs={{0,32},{32,64},{64,96},{96,128},{128,160},{160,192},{192,224},{224... | collective-permute-start | bytes 319496 | tf_op jit(solution)/shard_map/ppermute | solution.py:34
  70.1 5.4 %collective-permute-start.11 = (f32[26,8,128]{2,1,0:T(8,128)S(1)}, f32[26,8,128]{2,1,0:T(8,128)S(1)}, u32[]{:S(2)}, u32[]{:S(2)}) collective-permute-start(f32[26,8,128]{2,1,0:T(8,128)S(1)} %get-tuple-element.14), channel_id=1, source_target_pairs={{0,480},{32,0},{64,32},{96,64},{128,96},{160,128},{192,160},{224,1... | collective-permute-start | bytes 319496 | tf_op jit(solution)/shard_map/ppermute | solution.py:37
  76.2 19.6 %all-to-all-start = ((f32[4,13,8,128]{3,2,1,0:T(8,128)}), f32[4,13,8,128]{3,2,1,0:T(8,128)S(1)}, u32[]{:S(2)}, u32[]{:S(2)}) async-start(f32[4,13,8,128]{3,2,1,0:T(8,128)} %bitcast.23), calls=%async_computation | async-start | bytes 425984 | tf_op jit(solution)/shard_map/all_to_all | solution.py:100
  99.0 24.6 %all-to-all-start.1 = ((f32[64,8,128]{2,1,0:T(8,128)}), f32[64,8,128]{2,1,0:T(8,128)S(1)}, u32[]{:S(2)}, u32[]{:S(2)}) async-start(f32[64,8,128]{2,1,0:T(8,128)} %bitcast_select_fusion), calls=%async_computation.1 | async-start | bytes 524288 | tf_op jit(solution)/shard_map/all_to_all | solution.py:42
  147.6 18.6 %all-to-all-start.3 = ((f32[64,2,128]{2,1,0:T(2,128)}), f32[64,2,128]{2,1,0:T(2,128)S(1)}, u32[]{:S(2)}, u32[]{:S(2)}) async-start(f32[64,2,128]{2,1,0:T(2,128)} %bitcast.31), calls=%async_computation.3 | async-start | bytes 131072 | tf_op jit(solution)/shard_map/all_to_all | solution.py:42
  167.5 19.7 %all-to-all-start.4 = ((f32[64,4,128]{2,1,0:T(4,128)}), f32[64,4,128]{2,1,0:T(4,128)S(1)}, u32[]{:S(2)}, u32[]{:S(2)}) async-start(f32[64,4,128]{2,1,0:T(4,128)} %bitcast.34), calls=%async_computation.4 | async-start | bytes 262144 | tf_op jit(solution)/shard_map/all_to_all | solution.py:42

commit v2 on v1

--- a/solution.py
+++ b/solution.py
@@ -90,10 +90,11 @@
     held = exchanged(spread.reshape(islands, 2, LANES), ISLAND).reshape(-1, LANES)
     settled_out = rows_of(held, held_index.reshape(-1)).reshape(islands, 4, LANES)
     settled_in = exchanged(settled_out, ISLAND).reshape(-1, LANES)
-    settled_pages = rows_of(settled_in, source * 4 + slot)
 
     tiles = pseudo_grad[0].reshape(ROW_TILES, 8, GROUPS, NY, LANES).transpose(3, 0, 2, 1, 4)
     over_y = summed_around(tiles.reshape(NY, ROW_TILES * GROUPS, 8, LANES), "y", NY)
+    over_y, settled_in = lax.optimization_barrier((over_y, settled_in))
+    settled_pages = rows_of(settled_in, source * 4 + slot)
     classes = over_y.reshape(GROUPS, 4, 4, 8, LANES).transpose(2, 1, 0, 3, 4)
     windows = summed_around(classes.reshape(4, 4 * GROUPS, 8, LANES), "z", NZ).reshape(4, GROUPS, 8, LANES)
     far = [[4 * h + l for h in range(4)] for l in range(4)]

time: 191 us -> 181 us (0.948)
  waiting for transfers between devices: 70.7 us -> 46.8 us
  starting transfers between devices: 73.2 us -> 94.7 us
  blocking collectives: 19.5 us -> 0 us
  local copies, waits for them, and re-layouts: 9.66 us -> 18.2 us
  other arithmetic: 13.6 us -> 17.5 us
    all_to_all x3 -> x4, starting transfers between devices: 16.2 us -> 55.3 us  [exchanged(): return lax.all_to_all(array, axes, 0, 0, tiled=True)]
    all_to_all x1 -> x0, blocking collectives: 19.5 us -> none  [exchanged(): return lax.all_to_all(array, axes, 0, 0, tiled=True)]
    all_to_all x3 -> x4, waiting for transfers between devices: 43.8 us -> 30.7 us  [exchanged(): return lax.all_to_all(array, axes, 0, 0, tiled=True)]
    ppermute x2, starting transfers between devices: 12.9 us -> 7.44 us  [summed_around(): passed_down = lax.ppermute(far[half:], axis, down)]
    ppermute x2, waiting for transfers between devices: 7.59 us -> 2.37 us  [summed_around(): joined_down = lax.ppermute(below[half:] + passed_down, axis, down)]
    ppermute x2, waiting for transfers between devices: 5.53 us -> 1.32 us  [summed_around(): joined_up = lax.ppermute(above[:half] + passed_up, axis, up)]
    all_to_all x1, starting transfers between devices: 7.11 us -> 3.67 us  [body(): lax.all_to_all(windows, 'z', 0, 0, tiled=True, axis_index_groups=far)]
    ppermute x2, starting transfers between devices: 9.38 us -> 6.44 us  [summed_around(): passed_up = lax.ppermute(far[:half], axis, up)]
  transfers between devices with their start and end apart: 16 -> 17, of which waited for: 10 -> 6; matrix products, arithmetic and copies ran while one was open for 4% -> 14% of each run, Pallas kernels for 0% -> 0%
where the time goes in v2:
time: 181 us; the launch traced here: 179 us
  starting transfers between devices  94.7 us (52%)
  waiting for transfers between devices  46.8 us (26%)
  local copies, waits for them, and re-layouts  18.2 us (10%)
  other arithmetic  17.5 us (10%)
  between operations  1.96 us (1%)
    all_to_all x4, starting transfers between devices, exchanged(): return lax.all_to_all(array, axes, 0, 0, tiled=True)  55.3 us
    all_to_all x4, waiting for transfers between devices, exchanged(): return lax.all_to_all(array, axes, 0, 0, tiled=True)  30.7 us
    all_to_all x1, waiting for transfers between devices, body(): lax.all_to_all(windows, 'z', 0, 0, tiled=True, axis_index_groups=far)  12.4 us
    ppermute x2, starting transfers between devices, summed_around(): passed_down = lax.ppermute(far[half:], axis, down)  7.44 us
    ppermute x2, starting transfers between devices, summed_around(): joined_down = lax.ppermute(below[half:] + passed_down, axis, down)  7.39 us
    ppermute x2, starting transfers between devices, summed_around(): passed_up = lax.ppermute(far[:half], axis, up)  6.44 us
    ppermute x2, starting transfers between devices, summed_around(): near_down = lax.ppermute(below[:half], axis, down)  5.28 us
    ppermute x2, starting transfers between devices, summed_around(): joined_up = lax.ppermute(above[:half] + passed_up, axis, up)  5.28 us
  transfers between devices with their start and end apart: 17, of which 6 were waited for; matrix products, arithmetic and copies ran while one was open for 14% of the time, Pallas kernels for 0%

profile of v2, /device:TPU:1, one launch (start us, length us, event | category | flops | bytes accessed | tf_op | source)
XLA Modules:
  0.0 179.1 jit_solution(11544092475504919536)
XLA Ops:
  0.7 2.2 %copy.50 = f32[16,8,13,4,128]{4,1,2,0,3:T(8,128)S(1)} copy(f32[16,8,13,4,128]{4,1,3,2,0:T(8,128)} %bitcast.93) | data formatting | bytes 6815744 | tf_op jit(solution)/shard_map/reshape;squeeze | solution.py:94
  4.1 4.0 %collective-permute-start.1 = (f32[104,8,128]{2,1,0:T(8,128)}, f32[104,8,128]{2,1,0:T(8,128)}, u32[]{:S(2)}, u32[]{:S(2)}) collective-permute-start(f32[104,8,128]{2,1,0:T(8,128)} %get-tuple-element.14), channel_id=1, source_target_pairs={{0,8},{8,16},{16,24},{24,0},{1,9},{9,17},{17,25},{25,1},{2,10},{10... | collective-permute-start | bytes 1277960 | tf_op jit(solution)/shard_map/ppermute | solution.py:31
  8.2 3.4 %collective-permute-start = (f32[104,8,128]{2,1,0:T(8,128)}, f32[104,8,128]{2,1,0:T(8,128)}, u32[]{:S(2)}, u32[]{:S(2)}) collective-permute-start(f32[104,8,128]{2,1,0:T(8,128)} %get-tuple-element.13), channel_id=1, source_target_pairs={{0,24},{8,0},{16,8},{24,16},{1,25},{9,1},{17,9},{25,17},{2,26},{10... | collective-permute-start | bytes 1277960 | tf_op jit(solution)/shard_map/ppermute | solution.py:35
  11.5 3.4 %collective-permute-start.4 = (f32[104,8,128]{2,1,0:T(8,128)}, f32[104,8,128]{2,1,0:T(8,128)}, u32[]{:S(2)}, u32[]{:S(2)}) collective-permute-start(f32[104,8,128]{2,1,0:T(8,128)} %get-tuple-element.15), channel_id=1, source_target_pairs={{0,24},{8,0},{16,8},{24,16},{1,25},{9,1},{17,9},{25,17},{2,26},{10... | collective-permute-start | bytes 1277960 | tf_op jit(solution)/shard_map/ppermute | solution.py:32
  14.9 1.9 %collective-permute-start.3 = (f32[104,8,128]{2,1,0:T(8,128)}, f32[104,8,128]{2,1,0:T(8,128)}, u32[]{:S(2)}, u32[]{:S(2)}) collective-permute-start(f32[104,8,128]{2,1,0:T(8,128)} %get-tuple-element.16), channel_id=1, source_target_pairs={{0,8},{8,16},{16,24},{24,0},{1,9},{9,17},{17,25},{25,1},{2,10},{10... | collective-permute-start | bytes 1277960 | tf_op jit(solution)/shard_map/ppermute | solution.py:34
  18.4 1.8 %fusion.3 = f32[104,8,128]{2,1,0:T(8,128)} fusion(f32[104,8,128]{2,1,0:T(8,128)} %collective-permute-done.1, f32[4,208,8,128]{3,2,1,0:T(8,128)S(1)} %bitcast.89, s32[]{:T(128)S(6)} %select_n.419), kind=kLoop, calls=%fused_computation.14 | loop fusion | flops 106496 | bytes 1277956 | tf_op jit(solution)/shard_map/add | solution.py:36
  20.2 1.9 %collective-permute-start.2 = (f32[104,8,128]{2,1,0:T(8,128)}, f32[104,8,128]{2,1,0:T(8,128)}, u32[]{:S(2)}, u32[]{:S(2)}) collective-permute-start(f32[104,8,128]{2,1,0:T(8,128)} %fusion.3), channel_id=1, source_target_pairs={{0,8},{8,16},{16,24},{24,0},{1,9},{9,17},{17,25},{25,1},{2,10},{10... | collective-permute-start | bytes 1277960 | tf_op jit(solution)/shard_map/ppermute | solution.py:36
  23.0 19.4 %all-to-all-start = ((f32[64,2,128]{2,1,0:T(2,128)}), f32[64,2,128]{2,1,0:T(2,128)S(1)}, u32[]{:S(2)}, u32[]{:S(2)}) async-start(f32[64,2,128]{2,1,0:T(2,128)} %bitcast.13), calls=%async_computation | async-start | bytes 131072 | tf_op jit(solution)/shard_map/all_to_all | solution.py:42
  43.1 1.4 reduce-window.9
  52.4 2.3 %fusion.5 = (f32[104,8,128]{2,1,0:T(8,128)}, f32[104,8,128]{2,1,0:T(8,128)}) fusion(f32[104,8,128]{2,1,0:T(8,128)} %collective-permute-done.2, f32[104,8,128]{2,1,0:T(8,128)} %collective-permute-done, f32[4,208,8,128]{3,2,1,0:T(8,128)S(1)} %bitcast.90, s32[]{:T(128)S(6)} %select_n.415, f32[104,8,128]{2,1,0:T(8,128)} %collective-permute-done.4, ...), kind=kLoop, calls=%fused_computation.18 | loop fusion | flops 319488 | bytes 2981900 | tf_op jit(solution)/shard_map/add | solution.py:38
  54.7 4.1 %collective-permute-start.5 = (f32[104,8,128]{2,1,0:T(8,128)}, f32[104,8,128]{2,1,0:T(8,128)}, u32[]{:S(2)}, u32[]{:S(2)}) collective-permute-start(f32[104,8,128]{2,1,0:T(8,128)} %get-tuple-element.12), channel_id=1, source_target_pairs={{0,24},{8,0},{16,8},{24,16},{1,25},{9,1},{17,9},{25,17},{2,26},{10... | collective-permute-start | bytes 1277960 | tf_op jit(solution)/shard_map/ppermute | solution.py:37
  58.9 1.3 gather_fusion
  60.2 12.9 %all-to-all-start.1 = ((f32[64,4,128]{2,1,0:T(4,128)}), f32[64,4,128]{2,1,0:T(4,128)}, u32[]{:S(2)}, u32[]{:S(2)}) async-start(f32[64,4,128]{2,1,0:T(4,128)} %bitcast.99), calls=%async_computation.1 | async-start | bytes 262144 | tf_op jit(solution)/shard_map/all_to_all | solution.py:42
  73.2 1.2 fusion.2
  75.5 12.5 %all-to-all-done.1 = f32[64,4,128]{2,1,0:T(4,128)} async-done(((f32[64,4,128]{2,1,0:T(4,128)}), f32[64,4,128]{2,1,0:T(4,128)}, u32[]{:S(2)}, u32[]{:S(2)}) %all-to-all-start.1) | async-done | bytes 131104 | tf_op jit(solution)/shard_map/all_to_all | solution.py:42
  88.0 2.4 %collective-permute-start.7 = (f32[26,8,128]{2,1,0:T(8,128)S(1)}, f32[26,8,128]{2,1,0:T(8,128)S(1)}, u32[]{:S(2)}, u32[]{:S(2)}) collective-permute-start(f32[26,8,128]{2,1,0:T(8,128)S(1)} %get-tuple-element.20), channel_id=1, source_target_pairs={{0,32},{32,64},{64,96},{96,128},{128,160},{160,192},{192,224},{224... | collective-permute-start | bytes 319496 | tf_op jit(solution)/shard_map/ppermute | solution.py:31
  90.5 4.1 %collective-permute-start.10 = (f32[26,8,128]{2,1,0:T(8,128)S(1)}, f32[26,8,128]{2,1,0:T(8,128)S(1)}, u32[]{:S(2)}, u32[]{:S(2)}) collective-permute-start(f32[26,8,128]{2,1,0:T(8,128)S(1)} %get-tuple-element.21), channel_id=1, source_target_pairs={{0,480},{32,0},{64,32},{96,64},{128,96},{160,128},{192,160},{224,1... | collective-permute-start | bytes 319496 | tf_op jit(solution)/shard_map/ppermute | solution.py:32
  94.6 1.9 %collective-permute-start.6 = (f32[26,8,128]{2,1,0:T(8,128)S(1)}, f32[26,8,128]{2,1,0:T(8,128)S(1)}, u32[]{:S(2)}, u32[]{:S(2)}) collective-permute-start(f32[26,8,128]{2,1,0:T(8,128)S(1)} %get-tuple-element.19), channel_id=1, source_target_pairs={{0,480},{32,0},{64,32},{96,64},{128,96},{160,128},{192,160},{224,1... | collective-permute-start | bytes 319496 | tf_op jit(solution)/shard_map/ppermute | solution.py:35
  96.6 3.4 %collective-permute-start.8 = (f32[26,8,128]{2,1,0:T(8,128)S(1)}, f32[26,8,128]{2,1,0:T(8,128)S(1)}, u32[]{:S(2)}, u32[]{:S(2)}) collective-permute-start(f32[26,8,128]{2,1,0:T(8,128)S(1)} %fusion.9), channel_id=1, source_target_pairs={{0,32},{32,64},{64,96},{96,128},{128,160},{160,192},{192,224},{224... | collective-permute-start | bytes 319496 | tf_op jit(solution)/shard_map/ppermute | solution.py:36
  100.0 1.9 %collective-permute-start.9 = (f32[26,8,128]{2,1,0:T(8,128)S(1)}, f32[26,8,128]{2,1,0:T(8,128)S(1)}, u32[]{:S(2)}, u32[]{:S(2)}) collective-permute-start(f32[26,8,128]{2,1,0:T(8,128)S(1)} %get-tuple-element.22), channel_id=1, source_target_pairs={{0,32},{32,64},{64,96},{96,128},{128,160},{160,192},{192,224},{224... | collective-permute-start | bytes 319496 | tf_op jit(solution)/shard_map/ppermute | solution.py:34
  101.9 1.3 collective-permute-done.8
  103.3 3.3 %collective-permute-start.11 = (f32[26,8,128]{2,1,0:T(8,128)S(1)}, f32[26,8,128]{2,1,0:T(8,128)S(1)}, u32[]{:S(2)}, u32[]{:S(2)}) collective-permute-start(f32[26,8,128]{2,1,0:T(8,128)S(1)} %get-tuple-element.18), channel_id=1, source_target_pairs={{0,480},{32,0},{64,32},{96,64},{128,96},{160,128},{192,160},{224,1... | collective-permute-start | bytes 319496 | tf_op jit(solution)/shard_map/ppermute | solution.py:37
  106.7 2.4 %collective-permute-done.11 = f32[26,8,128]{2,1,0:T(8,128)S(1)} collective-permute-done((f32[26,8,128]{2,1,0:T(8,128)S(1)}, f32[26,8,128]{2,1,0:T(8,128)S(1)}, u32[]{:S(2)}, u32[]{:S(2)}) %collective-permute-start.11) | collective-permute-done | bytes 106528 | tf_op jit(solution)/shard_map/ppermute | solution.py:37
  109.7 3.7 %all-to-all-start.2 = ((f32[4,13,8,128]{3,2,1,0:T(8,128)}), f32[4,13,8,128]{3,2,1,0:T(8,128)S(1)}, u32[]{:S(2)}, u32[]{:S(2)}) async-start(f32[4,13,8,128]{3,2,1,0:T(8,128)} %bitcast.30), calls=%async_computation.2 | async-start | bytes 425984 | tf_op jit(solution)/shard_map/all_to_all | solution.py:101
  113.7 12.4 %all-to-all-done.2 = f32[4,13,8,128]{3,2,1,0:T(8,128)S(1)} async-done(((f32[4,13,8,128]{3,2,1,0:T(8,128)}), f32[4,13,8,128]{3,2,1,0:T(8,128)S(1)}, u32[]{:S(2)}, u32[]{:S(2)}) %all-to-all-start.2) | async-done | bytes 213024 | tf_op jit(solution)/shard_map/all_to_all | solution.py:101
  127.8 1.4 bitcast_select_fusion
  129.2 7.3 %all-to-all-start.3 = ((f32[64,8,128]{2,1,0:T(8,128)}), f32[64,8,128]{2,1,0:T(8,128)S(1)}, u32[]{:S(2)}, u32[]{:S(2)}) async-start(f32[64,8,128]{2,1,0:T(8,128)} %bitcast_select_fusion), calls=%async_computation.3 | async-start | bytes 524288 | tf_op jit(solution)/shard_map/all_to_all | solution.py:42
  137.9 1.6 gather_fusion.2
  139.5 14.5 %all-to-all-done.3 = f32[64,8,128]{2,1,0:T(8,128)S(1)} async-done(((f32[64,8,128]{2,1,0:T(8,128)}), f32[64,8,128]{2,1,0:T(8,128)S(1)}, u32[]{:S(2)}, u32[]{:S(2)}) %all-to-all-start.3) | async-done | bytes 262176 | tf_op jit(solution)/shard_map/all_to_all | solution.py:42
  154.7 1.2 broadcast_in_dim.81
  156.0 15.8 %all-to-all-start.4 = ((f32[8,1,1]{2,1,0:T(1,128)}), f32[8,1,1]{2,1,0:T(1,128)S(1)}, u32[]{:S(2)}, u32[]{:S(2)}) async-start(f32[8,1,1]{2,1,0:T(1,128)} %broadcast_in_dim.81), calls=%async_computation.4 | async-start | bytes 8192 | tf_op jit(solution)/shard_map/all_to_all | solution.py:42
  172.5 3.7 %all-to-all-done.4 = f32[8,1,1]{2,1,0:T(1,128)S(1)} async-done(((f32[8,1,1]{2,1,0:T(1,128)}), f32[8,1,1]{2,1,0:T(1,128)S(1)}, u32[]{:S(2)}, u32[]{:S(2)}) %all-to-all-start.4) | async-done | bytes 64 | tf_op jit(solution)/shard_map/all_to_all | solution.py:42
  (76 shorter events, 21.0 us)
Async XLA Ops:
  2.9 14.0 %copy-start = (f32[2,6656]{1,0:T(2,128)S(1)}, f32[2,6656]{1,0:T(2,128)}, u32[]{:S(2)}) copy-start(f32[2,6656]{1,0:T(2,128)} %param.6) | copy-start | bytes 159748
  2.9 14.0 %copy-start.1 = (f32[2,6656]{1,0:T(2,128)S(1)}, f32[2,6656]{1,0:T(2,128)}, u32[]{:S(2)}) copy-start(f32[2,6656]{1,0:T(2,128)} %param.7) | copy-start | bytes 159748
  2.9 39.5 %copy-start.3 = (s32[64]{0:T(128)S(1)}, s32[64]{0:T(128)}, u32[]{:S(2)}) copy-start(s32[64]{0:T(128)} %param.8) | copy-start | bytes 772
  2.9 42.5 %copy-start.4 = (s32[64]{0:T(128)S(1)}, s32[64]{0:T(128)}, u32[]{:S(2)}) copy-start(s32[64]{0:T(128)} %param.9) | copy-start | bytes 772
  4.1 14.3 %collective-permute-start.1 = (f32[104,8,128]{2,1,0:T(8,128)}, f32[104,8,128]{2,1,0:T(8,128)}, u32[]{:S(2)}, u32[]{:S(2)}) collective-permute-start(f32[104,8,128]{2,1,0:T(8,128)} %get-tuple-element.14), channel_id=1, source_target_pairs={{0,8},{8,16},{16,24},{24,0},{1,9},{9,17},{17,25},{25,1},{2,10},{10... | collective-permute-start | bytes 1277960 | tf_op jit(solution)/shard_map/ppermute | solution.py:31
  8.2 44.2 %collective-permute-start = (f32[104,8,128]{2,1,0:T(8,128)}, f32[104,8,128]{2,1,0:T(8,128)}, u32[]{:S(2)}, u32[]{:S(2)}) collective-permute-start(f32[104,8,128]{2,1,0:T(8,128)} %get-tuple-element.13), channel_id=1, source_target_pairs={{0,24},{8,0},{16,8},{24,16},{1,25},{9,1},{17,9},{25,17},{2,26},{10... | collective-permute-start | bytes 1277960 | tf_op jit(solution)/shard_map/ppermute | solution.py:35
  11.5 40.8 %collective-permute-start.4 = (f32[104,8,128]{2,1,0:T(8,128)}, f32[104,8,128]{2,1,0:T(8,128)}, u32[]{:S(2)}, u32[]{:S(2)}) collective-permute-start(f32[104,8,128]{2,1,0:T(8,128)} %get-tuple-element.15), channel_id=1, source_target_pairs={{0,24},{8,0},{16,8},{24,16},{1,25},{9,1},{17,9},{25,17},{2,26},{10... | collective-permute-start | bytes 1277960 | tf_op jit(solution)/shard_map/ppermute | solution.py:32
  14.9 58.2 %collective-permute-start.3 = (f32[104,8,128]{2,1,0:T(8,128)}, f32[104,8,128]{2,1,0:T(8,128)}, u32[]{:S(2)}, u32[]{:S(2)}) collective-permute-start(f32[104,8,128]{2,1,0:T(8,128)} %get-tuple-element.16), channel_id=1, source_target_pairs={{0,8},{8,16},{16,24},{24,0},{1,9},{9,17},{17,25},{25,1},{2,10},{10... | collective-permute-start | bytes 1277960 | tf_op jit(solution)/shard_map/ppermute | solution.py:34
  20.2 32.1 %collective-permute-start.2 = (f32[104,8,128]{2,1,0:T(8,128)}, f32[104,8,128]{2,1,0:T(8,128)}, u32[]{:S(2)}, u32[]{:S(2)}) collective-permute-start(f32[104,8,128]{2,1,0:T(8,128)} %fusion.3), channel_id=1, source_target_pairs={{0,8},{8,16},{16,24},{24,0},{1,9},{9,17},{17,25},{25,1},{2,10},{10... | collective-permute-start | bytes 1277960 | tf_op jit(solution)/shard_map/ppermute | solution.py:36
  23.0 35.9 %all-to-all-start = ((f32[64,2,128]{2,1,0:T(2,128)}), f32[64,2,128]{2,1,0:T(2,128)S(1)}, u32[]{:S(2)}, u32[]{:S(2)}) async-start(f32[64,2,128]{2,1,0:T(2,128)} %bitcast.13), calls=%async_computation | async-start | bytes 131072 | tf_op jit(solution)/shard_map/all_to_all | solution.py:42
  54.7 18.4 %collective-permute-start.5 = (f32[104,8,128]{2,1,0:T(8,128)}, f32[104,8,128]{2,1,0:T(8,128)}, u32[]{:S(2)}, u32[]{:S(2)}) collective-permute-start(f32[104,8,128]{2,1,0:T(8,128)} %get-tuple-element.12), channel_id=1, source_target_pairs={{0,24},{8,0},{16,8},{24,16},{1,25},{9,1},{17,9},{25,17},{2,26},{10... | collective-permute-start | bytes 1277960 | tf_op jit(solution)/shard_map/ppermute | solution.py:37
  60.2 27.7 %all-to-all-start.1 = ((f32[64,4,128]{2,1,0:T(4,128)}), f32[64,4,128]{2,1,0:T(4,128)}, u32[]{:S(2)}, u32[]{:S(2)}) async-start(f32[64,4,128]{2,1,0:T(4,128)} %bitcast.99), calls=%async_computation.1 | async-start | bytes 262144 | tf_op jit(solution)/shard_map/all_to_all | solution.py:42
  88.0 8.5 %collective-permute-start.7 = (f32[26,8,128]{2,1,0:T(8,128)S(1)}, f32[26,8,128]{2,1,0:T(8,128)S(1)}, u32[]{:S(2)}, u32[]{:S(2)}) collective-permute-start(f32[26,8,128]{2,1,0:T(8,128)S(1)} %get-tuple-element.20), channel_id=1, source_target_pairs={{0,32},{32,64},{64,96},{96,128},{128,160},{160,192},{192,224},{224... | collective-permute-start | bytes 319496 | tf_op jit(solution)/shard_map/ppermute | solution.py:31
  90.5 11.4 %collective-permute-start.10 = (f32[26,8,128]{2,1,0:T(8,128)S(1)}, f32[26,8,128]{2,1,0:T(8,128)S(1)}, u32[]{:S(2)}, u32[]{:S(2)}) collective-permute-start(f32[26,8,128]{2,1,0:T(8,128)S(1)} %get-tuple-element.21), channel_id=1, source_target_pairs={{0,480},{32,0},{64,32},{96,64},{128,96},{160,128},{192,160},{224,1... | collective-permute-start | bytes 319496 | tf_op jit(solution)/shard_map/ppermute | solution.py:32
  94.6 7.3 %collective-permute-start.6 = (f32[26,8,128]{2,1,0:T(8,128)S(1)}, f32[26,8,128]{2,1,0:T(8,128)S(1)}, u32[]{:S(2)}, u32[]{:S(2)}) collective-permute-start(f32[26,8,128]{2,1,0:T(8,128)S(1)} %get-tuple-element.19), channel_id=1, source_target_pairs={{0,480},{32,0},{64,32},{96,64},{128,96},{160,128},{192,160},{224,1... | collective-permute-start | bytes 319496 | tf_op jit(solution)/shard_map/ppermute | solution.py:35
  96.6 6.7 %collective-permute-start.8 = (f32[26,8,128]{2,1,0:T(8,128)S(1)}, f32[26,8,128]{2,1,0:T(8,128)S(1)}, u32[]{:S(2)}, u32[]{:S(2)}) collective-permute-start(f32[26,8,128]{2,1,0:T(8,128)S(1)} %fusion.9), channel_id=1, source_target_pairs={{0,32},{32,64},{64,96},{96,128},{128,160},{160,192},{192,224},{224... | collective-permute-start | bytes 319496 | tf_op jit(solution)/shard_map/ppermute | solution.py:36
  100.0 6.7 %collective-permute-start.9 = (f32[26,8,128]{2,1,0:T(8,128)S(1)}, f32[26,8,128]{2,1,0:T(8,128)S(1)}, u32[]{:S(2)}, u32[]{:S(2)}) collective-permute-start(f32[26,8,128]{2,1,0:T(8,128)S(1)} %get-tuple-element.22), channel_id=1, source_target_pairs={{0,32},{32,64},{64,96},{96,128},{128,160},{160,192},{192,224},{224... | collective-permute-start | bytes 319496 | tf_op jit(solution)/shard_map/ppermute | solution.py:34
  103.3 5.7 %collective-permute-start.11 = (f32[26,8,128]{2,1,0:T(8,128)S(1)}, f32[26,8,128]{2,1,0:T(8,128)S(1)}, u32[]{:S(2)}, u32[]{:S(2)}) collective-permute-start(f32[26,8,128]{2,1,0:T(8,128)S(1)} %get-tuple-element.18), channel_id=1, source_target_pairs={{0,480},{32,0},{64,32},{96,64},{128,96},{160,128},{192,160},{224,1... | collective-permute-start | bytes 319496 | tf_op jit(solution)/shard_map/ppermute | solution.py:37
  109.7 67.9 %copy-start.2 = (f32[2,6656]{1,0:T(2,128)S(1)}, f32[2,6656]{1,0:T(2,128)}, u32[]{:S(2)}) copy-start(f32[2,6656]{1,0:T(2,128)} %param.7) | copy-start | bytes 159748
  109.7 16.4 %all-to-all-start.2 = ((f32[4,13,8,128]{3,2,1,0:T(8,128)}), f32[4,13,8,128]{3,2,1,0:T(8,128)S(1)}, u32[]{:S(2)}, u32[]{:S(2)}) async-start(f32[4,13,8,128]{3,2,1,0:T(8,128)} %bitcast.30), calls=%async_computation.2 | async-start | bytes 425984 | tf_op jit(solution)/shard_map/all_to_all | solution.py:101
  129.2 24.9 %all-to-all-start.3 = ((f32[64,8,128]{2,1,0:T(8,128)}), f32[64,8,128]{2,1,0:T(8,128)S(1)}, u32[]{:S(2)}, u32[]{:S(2)}) async-start(f32[64,8,128]{2,1,0:T(8,128)} %bitcast_select_fusion), calls=%async_computation.3 | async-start | bytes 524288 | tf_op jit(solution)/shard_map/all_to_all | solution.py:42
  156.0 20.3 %all-to-all-start.4 = ((f32[8,1,1]{2,1,0:T(1,128)}), f32[8,1,1]{2,1,0:T(1,128)S(1)}, u32[]{:S(2)}, u32[]{:S(2)}) async-start(f32[8,1,1]{2,1,0:T(1,128)} %broadcast_in_dim.81), calls=%async_computation.4 | async-start | bytes 8192 | tf_op jit(solution)/shard_map/all_to_all | solution.py:42

commit v3 on v1

v3 whole, which is shorter than its diff:
```python
import jax
import jax.numpy as jnp
from jax import lax
from jax.experimental import pallas as pl
from jax.experimental.pallas import tpu as pltpu
from jax.sharding import Mesh
from jax.sharding import PartitionSpec as P

ISLAND = ("z", "y")
TENSOR = ("x", "core")

epsilon = 1e-06
decay_rate = 0.9
outer_rate = 0.7

NZ, NY, ROW_TILES, GROUPS, LANES = 16, 4, 16, 13, 128
PER_ROW = NY * GROUPS
IN_VMEM = pl.BlockSpec(memory_space=pltpu.VMEM)
ROWS_SENT, HELD_FROM, PART_AT = 12, 104, 232


def shift(n, by):
    return [(i, (i + by) % n) for i in range(n)]


def pick(array, index, axis_size):
    return lax.dynamic_index_in_dim(array, index % axis_size, 0, keepdims=False)


def summed_around(class_of, riders, axis, n):
    here = lax.axis_index(axis)
    far = class_of(here + 2)
    half = far.shape[0] // 2
    up, down = shift(n, 1), shift(n, -1)
    join = lambda *parts: jnp.concatenate(parts, axis=0)
    passed_up = lax.ppermute(join(far[:half], pick(riders, here + 2, n)), axis, up)
    passed_down = lax.ppermute(far[half:], axis, down)
    above, below, own = class_of(here + 1), class_of(here + 3), class_of(here)
    near_up = lax.ppermute(join(above[half:], pick(riders, here + 1, n)), axis, up)
    near_down = lax.ppermute(join(below[:half], pick(riders, here + 3, n)), axis, down)
    for_above, for_below = lax.optimization_barrier(
        (join(above[:half] + passed_up[:half], passed_up[half:]), below[half:] + passed_down)
    )
    joined_up = lax.ppermute(for_above, axis, up)
    joined_down = lax.ppermute(for_below, axis, down)
    own, near_up, near_down, joined_up, joined_down = lax.optimization_barrier(
        (own, near_up, near_down, joined_up, joined_down)
    )
    total = join(own[:half] + near_down[:half] + joined_up[:half], own[half:] + near_up[:half] + joined_down)
    senders = jnp.stack([pick(riders, here, n), near_down[half:], joined_up[half:], near_up[half:]])
    return total, rolled(senders, n - here)


def summed_in_window(classes, riders, axis, n):
    here = lax.axis_index(axis)
    half, whole = classes.shape[1] // 2, classes.shape[1]
    join = lambda *parts: jnp.concatenate(parts, axis=0)
    far = pick(classes, here + 2, 4)
    far_up = lax.ppermute(join(far[:half], pick(riders, here + 2, 4)), axis, shift(n, 2))
    far_down = lax.ppermute(far[half:], axis, shift(n, -2))
    near_up = lax.ppermute(join(pick(classes, here + 1, 4), pick(riders, here + 1, 4)), axis, shift(n, 1))
    near_down = lax.ppermute(join(pick(classes, here + 3, 4), pick(riders, here + 3, 4)), axis, shift(n, -1))
    return pl.pallas_call(
        window_kernel,
        out_shape=jax.ShapeDtypeStruct((4, GROUPS + 4, 8, LANES), jnp.float32),
        in_specs=[IN_VMEM] * 6,
        out_specs=IN_VMEM,
        compiler_params=pltpu.CompilerParams(vmem_limit_bytes=4 << 20),
    )(pick(classes, here, 4), pick(riders, here, 4), near_up, near_down, far_up, far_down)


def window_kernel(own, rider, near_up, near_down, far_up, far_down, out):
    for chunk in range(4):
        at = pl.ds(GROUPS * chunk, GROUPS)
        far = far_up if chunk < 2 else far_down
        out[chunk, :GROUPS] = own[at] + near_up[at] + near_down[at] + far[pl.ds(GROUPS * (chunk % 2), GROUPS)]
        out[chunk, GROUPS] = rider[chunk]
        out[chunk, GROUPS + 1] = near_up[4 * GROUPS + chunk]
        out[chunk, GROUPS + 2] = near_down[4 * GROUPS + chunk]
        out[chunk, GROUPS + 3] = far_up[2 * GROUPS + chunk]


def table_kernel(windows, out):
    mean = (windows[0, :GROUPS] + windows[1, :GROUPS] + windows[2, :GROUPS] + windows[3, :GROUPS]) / (NZ * NY)
    out[:GROUPS] = mean
    for chunk in range(4):
        out[pl.ds(GROUPS + 4 * chunk, 4)] = windows[chunk, GROUPS:]
    out[GROUPS + 16] = jnp.full((8, LANES), jnp.sum(mean * mean), jnp.float32)


def rolled(array, by):
    n = array.shape[0]
    return lax.dynamic_slice_in_dim(jnp.concatenate([array, array], axis=0), by % n, n, 0)


def exchanged(array, axes):
    return lax.all_to_all(array, axes, 0, 0, tiled=True)


def rows_of(array, index):
    return array.at[index].get(mode="promise_in_bounds")


def body(pseudo_grad, outer_params, momentum, save_pages, writer):
    z, y = lax.axis_index("z"), lax.axis_index("y")
    islands = NZ * NY
    entries = pseudo_grad.shape[1] * pseudo_grad.shape[2] * lax.axis_size(TENSOR)

    order = jnp.arange(islands, dtype=jnp.int32)[:, None]

    def window_of(target):
        hit = writer[:, None] == target[None, :]
        position = jnp.sum(jnp.where(hit, order, 0), axis=0)
        length = jnp.sum(jnp.where(hit, save_pages[:, None], 0), axis=0)
        return jnp.sum(jnp.where(order < position[None, :], save_pages[:, None], 0), axis=0), length

    def page_for(target, slot):
        start, length = window_of(target)
        first_row = start // PER_ROW
        near_row = first_row + (slot - first_row) % 4
        held, local = jnp.zeros_like(target), jnp.zeros_like(target)
        for row in (near_row, near_row + 4):
            tile = GROUPS * (row // 8)
            group = (z - tile) % NZ
            page = PER_ROW * row + NY * group + y
            inside = (group < GROUPS) & (page >= start) & (page < start + length)
            apart = (row // 8 - z % 4) % NZ
            sender = jnp.where(apart % 4 == 0, 0, jnp.where(apart % 4 == 1, 2, jnp.where(apart % 4 == 2, 3, 1)))
            held = jnp.where(inside, 32 * ((apart + 2) // 4 % 4) + 8 * sender + row % 8, held)
            local = jnp.where(inside, 8 * ((tile + group) // NZ) + row % 8, local)
        return held, local

    flat = jnp.arange(ROWS_SENT * islands, dtype=jnp.int32)
    target, kind = flat // ROWS_SENT, flat % ROWS_SENT
    held_index, sum_index = page_for(target, kind % 4)
    tile = GROUPS * (target // NY)
    group = (z - tile) % NZ
    row_index = jnp.where(group < GROUPS, 8 * ((tile + group) // NZ), 0) + 2 * (target % NY) + kind % 2
    send_index = jnp.where(kind < 4, sum_index, jnp.where(kind < 8, HELD_FROM + held_index, row_index))
    send_index = jnp.where(kind < 10, send_index, PART_AT)
    own_start, own_length = window_of((z * NY + y)[None])
    place = jnp.arange(208, dtype=jnp.int32)
    page = jnp.minimum(own_start + place, 6655)
    row, block = page // PER_ROW, page % PER_ROW
    source = ((GROUPS * (row // 8) + block // NY) % NZ) * NY + block % NY
    slot = row % 4

    settled = outer_params - (outer_rate * decay_rate * decay_rate) * momentum
    settled = settled.reshape(2, GROUPS, NY, LANES).transpose(2, 1, 0, 3)
    settled = jnp.concatenate([settled, jnp.zeros((NY, NZ - GROUPS, 2, LANES), jnp.float32)], axis=1)

    by_block = pseudo_grad[0].reshape(ROW_TILES, 8, GROUPS, NY, LANES)

    def block_class(index):
        taken = lax.dynamic_index_in_dim(by_block, index % NY, 3, keepdims=False)
        return taken.transpose(0, 2, 1, 3).reshape(ROW_TILES * GROUPS, 8, LANES)

    over_y, settled = summed_around(block_class, settled.reshape(NY, 4, 8, LANES), "y", NY)
    settled = settled.reshape(NY, NZ, 2, LANES).transpose(1, 0, 2, 3).reshape(NZ, 8, LANES)
    settled = rolled(settled, -GROUPS * z).reshape(4, 4, 8, LANES).transpose(1, 0, 2, 3)
    classes = over_y.reshape(GROUPS, 4, 4, 8, LANES).transpose(2, 1, 0, 3, 4)
    windows = summed_in_window(classes.reshape(4, 4 * GROUPS, 8, LANES), settled, "z", NZ)
    far = [[4 * h + l for h in range(4)] for l in range(4)]
    windows = lax.all_to_all(windows, "z", 0, 0, tiled=True, axis_index_groups=far)
    table = pl.pallas_call(
        table_kernel,
        out_shape=jax.ShapeDtypeStruct((GROUPS + 17, 8, LANES), jnp.float32),
        in_specs=[IN_VMEM],
        out_specs=IN_VMEM,
        compiler_params=pltpu.CompilerParams(vmem_limit_bytes=4 << 20),
    )(windows).reshape(-1, LANES)

    outgoing = rows_of(table, send_index).reshape(-1, 4, LANES)
    arrived = exchanged(outgoing, ISLAND).reshape(islands, 3, 4, LANES)
    over_islands = jnp.sum(arrived[:, 2, 2], axis=0)
    eight = exchanged(jnp.broadcast_to(over_islands, (lax.axis_size(TENSOR), 1, LANES)), TENSOR)
    square_sum = jnp.sum(eight, axis=0)
    scale = 1.0 / jnp.sqrt(square_sum / entries + epsilon)

    mine = arrived[:, 2, :2].reshape(NZ, NY, 2, LANES)
    mine = lax.dynamic_slice_in_dim(jnp.concatenate([mine, mine], axis=0), (GROUPS * z) % NZ, GROUPS, 0)
    normed = (mine.transpose(2, 0, 1, 3) * scale).reshape(2, -1)
    new_momentum = decay_rate * momentum + normed
    new_master = outer_params - outer_rate * (normed + decay_rate * new_momentum)
    arrived = arrived.reshape(-1, LANES)
    gradient_pages = rows_of(arrived, source * ROWS_SENT + slot)
    settled_pages = rows_of(arrived, source * ROWS_SENT + 4 + slot)
    pages = settled_pages - (outer_rate * (1.0 + decay_rate)) * (gradient_pages * scale)
    packed = jnp.where((place < own_length)[:, None], pages, 0.0).astype(jnp.bfloat16)
    return (new_master, new_momentum, packed[None])


def solution(mesh):
    split = Mesh(mesh.devices.reshape(NZ, NY, 4, 2), ("z", "y", "x", "core"))
    return jax.shard_map(
        body,
        mesh=split,
        in_specs=(P(ISLAND, None, TENSOR), P(ISLAND, TENSOR), P(ISLAND, TENSOR), P(), P()),
        out_specs=(P(ISLAND, TENSOR), P(ISLAND, TENSOR), P(ISLAND, None, TENSOR)),
        check_vma=False,
    )
```

time: 191 us -> 141 us (0.74); the launches traced: 189 us -> 141 us
  waiting for transfers between devices: 70.7 us -> 50.4 us
  blocking collectives: 19.5 us -> 0 us
  other arithmetic: 13.6 us -> 8.44 us
    all_to_all x3 -> x2, waiting for transfers between devices: 43.8 us -> 22.9 us  [exchanged(): return lax.all_to_all(array, axes, 0, 0, tiled=True)]
    all_to_all x1 -> x0, blocking collectives: 19.5 us -> none  [exchanged(): return lax.all_to_all(array, axes, 0, 0, tiled=True)]
    ppermute x2 -> x1, starting transfers between devices: 12.9 us -> 3.36 us  [summed_around(): passed_down = lax.ppermute(far[half:], axis, down)]
    all_to_all x3 -> x2, starting transfers between devices: 16.2 us -> 21.2 us  [exchanged(): return lax.all_to_all(array, axes, 0, 0, tiled=True)]
    ppermute x10 -> x9, starting transfers between devices: 37 us -> 40.3 us  [the longest x1 13.7 us: summed_in_window(): lax.ppermute(join(pick(classes, here + 3, 4), pick(riders, here + 3, 4)),...]
    all_to_all x1, waiting for transfers between devices: 12.3 us -> 15.4 us  [body(): lax.all_to_all(windows, 'z', 0, 0, tiled=True, axis_index_groups=far)]
    add x8 -> x3, other arithmetic: 4.43 us -> 1.97 us  [the longest x1 1.12 us: summed_around(): own[:half] + near_down[:half] + joined_up[:half]]
    another operation x2 -> x0, local copies, waits for them, and re-layouts: 2.28 us -> none  [the longest x1 2.18 us: body(): pseudo_grad[0].reshape(ROW_TILES, 8, GROUPS, NY, LANES)]
  transfers between devices with their start and end apart: 16 -> 13, of which waited for: 10 -> 5; matrix products, arithmetic and copies ran while one was open for 4% -> 5% of each run, Pallas kernels for 0% -> 0%
where the time goes in v3:
time: 141 us
  starting transfers between devices  71.5 us (51%)
  waiting for transfers between devices  50.4 us (36%)
  other arithmetic  8.44 us (6%)
  local copies, waits for them, and re-layouts  7.89 us (6%)
    all_to_all x2, waiting for transfers between devices, exchanged(): return lax.all_to_all(array, axes, 0, 0, tiled=True)  22.9 us
    all_to_all x2, starting transfers between devices, exchanged(): return lax.all_to_all(array, axes, 0, 0, tiled=True)  21.2 us
    all_to_all x1, waiting for transfers between devices, body(): lax.all_to_all(windows, 'z', 0, 0, tiled=True, axis_index_groups=far)  15.4 us
    ppermute x1, starting transfers between devices, summed_in_window(): lax.ppermute(join(pick(classes, here + 3, 4), pick(riders, here + 3, 4)),...  13.7 us
    ppermute x1, waiting for transfers between devices, summed_around(): joined_down = lax.ppermute(for_below, axis, down)  9.36 us
    all_to_all x1, starting transfers between devices, body(): lax.all_to_all(windows, 'z', 0, 0, tiled=True, axis_index_groups=far)  6.62 us
    ppermute x1, starting transfers between devices, summed_around(): joined_up = lax.ppermute(for_above, axis, up)  6.06 us
    ppermute x1, starting transfers between devices, summed_in_window(): far_down = lax.ppermute(far[half:], axis, shift(n, -2))  5.47 us
  transfers between devices with their start and end apart: 13, of which 5 were waited for; matrix products, arithmetic and copies ran while one was open for 5% of the time, Pallas kernels for 0%

profile of v3, /device:TPU:1, one launch (start us, length us, event | category | flops | bytes accessed | tf_op | source)
XLA Modules:
  0.0 140.5 jit_solution(14257307299897122805)
XLA Ops:
  0.7 2.2 %dynamic-slice_bitcast_fusion = (f32[16,13,8,128]{3,2,1,0:T(8,128)S(1)}, f32[16,13,8,128]{3,2,1,0:T(8,128)S(1)}, f32[16,13,8,128]{3,2,1,0:T(8,128)S(1)}, f32[16,8,13,1,128]{4,1,3,2,0:T(8,128)S(1)}) fusion(f32[16,8,13,4,128]{4,1,3,2,0:T(8,128)} %bitcast.99, s32[]{:T(128)S(6)} %select_n.745, s32[]{:T(128)S(6)} %select_n.743, s32[]{:T(128)S(6)} %select_n.741, ...), kind=kLoop, calls=%fused_computation.4 | loop fusion | bytes 6815760 | tf_op jit(solution)/shard_map/transpose | solution.py:156
  2.9 0.8 fusion.47
  4.0 4.0 %collective-permute-start.2 = (f32[108,8,128]{2,1,0:T(8,128)S(1)}, f32[108,8,128]{2,1,0:T(8,128)S(1)}, u32[]{:S(2)}, u32[]{:S(2)}) collective-permute-start(f32[108,8,128]{2,1,0:T(8,128)S(1)} %pad_maximum_fusion.3), channel_id=1, source_target_pairs={{0,8},{8,16},{16,24},{24,0},{1,9},{9,17},{17,25},{25,1},{2,10},{10... | collective-permute-start | bytes 1327112 | tf_op jit(solution)/shard_map/ppermute | solution.py:36
  8.0 3.4 %collective-permute-start.3 = (f32[104,8,128]{2,1,0:T(8,128)}, f32[104,8,128]{2,1,0:T(8,128)S(1)}, u32[]{:S(2)}, u32[]{:S(2)}) collective-permute-start(f32[104,8,128]{2,1,0:T(8,128)} %bitcast.23), channel_id=1, source_target_pairs={{0,24},{8,0},{16,8},{24,16},{1,25},{9,1},{17,9},{25,17},{2,26},{10... | collective-permute-start | bytes 1277960 | tf_op jit(solution)/shard_map/ppermute | solution.py:37
  11.5 3.4 %collective-permute-start.1 = (f32[108,8,128]{2,1,0:T(8,128)S(1)}, f32[108,8,128]{2,1,0:T(8,128)S(1)}, u32[]{:S(2)}, u32[]{:S(2)}) collective-permute-start(f32[108,8,128]{2,1,0:T(8,128)S(1)} %pad_maximum_fusion.2), channel_id=1, source_target_pairs={{0,24},{8,0},{16,8},{24,16},{1,25},{9,1},{17,9},{25,17},{2,26},{10... | collective-permute-start | bytes 1327112 | tf_op jit(solution)/shard_map/ppermute | solution.py:40
  14.9 0.8 pad_maximum_fusion.1
  15.7 1.9 %collective-permute-start = (f32[108,8,128]{2,1,0:T(8,128)}, f32[108,8,128]{2,1,0:T(8,128)S(1)}, u32[]{:S(2)}, u32[]{:S(2)}) collective-permute-start(f32[108,8,128]{2,1,0:T(8,128)} %pad_maximum_fusion.1), channel_id=1, source_target_pairs={{0,8},{8,16},{16,24},{24,0},{1,9},{9,17},{17,25},{25,1},{2,10},{10... | collective-permute-start | bytes 1327112 | tf_op jit(solution)/shard_map/ppermute | solution.py:39
  17.7 0.8 bitcast_add_fusion
  18.5 6.1 %collective-permute-start.4 = (f32[108,8,128]{2,1,0:T(8,128)S(1)}, f32[108,8,128]{2,1,0:T(8,128)S(1)}, u32[]{:S(2)}, u32[]{:S(2)}) collective-permute-start(f32[108,8,128]{2,1,0:T(8,128)S(1)} %pad_maximum_fusion.4), channel_id=1, source_target_pairs={{0,8},{8,16},{16,24},{24,0},{1,9},{9,17},{17,25},{25,1},{2,10},{10... | collective-permute-start | bytes 1327112 | tf_op jit(solution)/shard_map/ppermute | solution.py:44
  24.6 1.9 %collective-permute-start.5 = (f32[104,8,128]{2,1,0:T(8,128)}, f32[104,8,128]{2,1,0:T(8,128)}, u32[]{:S(2)}, u32[]{:S(2)}) collective-permute-start(f32[104,8,128]{2,1,0:T(8,128)} %bitcast_add_fusion), channel_id=1, source_target_pairs={{0,24},{8,0},{16,8},{24,16},{1,25},{9,1},{17,9},{25,17},{2,26},{10... | collective-permute-start | bytes 1277960 | tf_op jit(solution)/shard_map/ppermute | solution.py:45
  26.7 9.4 %collective-permute-done.5 = f32[104,8,128]{2,1,0:T(8,128)} collective-permute-done((f32[104,8,128]{2,1,0:T(8,128)}, f32[104,8,128]{2,1,0:T(8,128)}, u32[]{:S(2)}, u32[]{:S(2)}) %collective-permute-start.5) | collective-permute-done | bytes 426016 | tf_op jit(solution)/shard_map/ppermute | solution.py:45
  36.2 1.1 slice_add_fusion.1
  37.6 13.7 %collective-permute-start.7 = (f32[56,8,128]{2,1,0:T(8,128)S(1)}, f32[56,8,128]{2,1,0:T(8,128)S(1)}, u32[]{:S(2)}, u32[]{:S(2)}) collective-permute-start(f32[56,8,128]{2,1,0:T(8,128)S(1)} %pad_maximum_fusion.6), channel_id=1, source_target_pairs={{0,480},{32,0},{64,32},{96,64},{128,96},{160,128},{192,160},{224,1... | collective-permute-start | bytes 688136 | tf_op jit(solution)/shard_map/ppermute | solution.py:62
  51.4 1.9 %collective-permute-start.6 = (f32[56,8,128]{2,1,0:T(8,128)S(1)}, f32[56,8,128]{2,1,0:T(8,128)S(1)}, u32[]{:S(2)}, u32[]{:S(2)}) collective-permute-start(f32[56,8,128]{2,1,0:T(8,128)S(1)} %pad_maximum_fusion.5), channel_id=1, source_target_pairs={{0,32},{32,64},{64,96},{96,128},{128,160},{160,192},{192,224},{224... | collective-permute-start | bytes 688136 | tf_op jit(solution)/shard_map/ppermute | solution.py:61
  53.4 1.9 %collective-permute-start.8 = (f32[30,8,128]{2,1,0:T(8,128)S(1)}, f32[30,8,128]{2,1,0:T(8,128)S(1)}, u32[]{:S(2)}, u32[]{:S(2)}) collective-permute-start(f32[30,8,128]{2,1,0:T(8,128)S(1)} %pad_maximum_fusion.7), channel_id=1, source_target_pairs={{0,64},{32,96},{64,128},{96,160},{128,192},{160,224},{192,256},{22... | collective-permute-start | bytes 368648 | tf_op jit(solution)/shard_map/ppermute | solution.py:59
  55.3 5.5 %collective-permute-start.9 = (f32[26,8,128]{2,1,0:T(8,128)S(1)}, f32[26,8,128]{2,1,0:T(8,128)S(1)}, u32[]{:S(2)}, u32[]{:S(2)}) collective-permute-start(f32[26,8,128]{2,1,0:T(8,128)S(1)} %get-tuple-element.27), channel_id=1, source_target_pairs={{0,448},{32,480},{64,0},{96,32},{128,64},{160,96},{192,128},{224,1... | collective-permute-start | bytes 319496 | tf_op jit(solution)/shard_map/ppermute | solution.py:60
  60.8 2.8 %collective-permute-done.9.far_down = f32[26,8,128]{2,1,0:T(8,128)S(1)} collective-permute-done((f32[26,8,128]{2,1,0:T(8,128)S(1)}, f32[26,8,128]{2,1,0:T(8,128)S(1)}, u32[]{:S(2)}, u32[]{:S(2)}) %collective-permute-start.9) | collective-permute-done | bytes 106528 | tf_op jit(solution)/shard_map/ppermute | solution.py:60
  63.5 0.8 shard_map.76
  64.3 6.6 %all-to-all-start = ((f32[4,17,8,128]{3,2,1,0:T(8,128)}), f32[4,17,8,128]{3,2,1,0:T(8,128)S(1)}, u32[]{:S(2)}, u32[]{:S(2)}) async-start(f32[4,17,8,128]{3,2,1,0:T(8,128)} %shard_map.76), calls=%async_computation | async-start | bytes 557056 | tf_op jit(solution)/shard_map/all_to_all | solution.py:164
  71.5 15.4 %all-to-all-done.windows = f32[4,17,8,128]{3,2,1,0:T(8,128)S(1)} async-done(((f32[4,17,8,128]{3,2,1,0:T(8,128)}), f32[4,17,8,128]{3,2,1,0:T(8,128)S(1)}, u32[]{:S(2)}, u32[]{:S(2)}) %all-to-all-start) | async-done | bytes 278560 | tf_op jit(solution)/shard_map/all_to_all | solution.py:164
  87.1 2.3 %gather_fusion = f32[768,128]{1,0:T(8,128)} fusion(f32[240,128]{1,0:T(8,128)S(1)} %bitcast.94, s32[1024]{0:T(1024)S(1)} %pad_clamp_fusion.2), kind=kCustom, calls=%fused_computation | custom fusion | bytes 789504 | tf_op jit(solution)/shard_map/gather | solution.py:101
  89.3 11.5 %all-to-all-start.1 = ((f32[192,4,128]{2,1,0:T(4,128)}), f32[192,4,128]{2,1,0:T(4,128)S(1)}, u32[]{:S(2)}, u32[]{:S(2)}) async-start(f32[192,4,128]{2,1,0:T(4,128)} %bitcast.44), calls=%async_computation.1 | async-start | bytes 786432 | tf_op jit(solution)/shard_map/all_to_all | solution.py:97
  101.5 1.3 fusion.45
  102.7 0.7 compare_select_fusion.60
  103.5 20.5 %all-to-all-done.1 = f32[192,4,128]{2,1,0:T(4,128)S(1)} async-done(((f32[192,4,128]{2,1,0:T(4,128)}), f32[192,4,128]{2,1,0:T(4,128)S(1)}, u32[]{:S(2)}, u32[]{:S(2)}) %all-to-all-start.1) | async-done | bytes 393248 | tf_op jit(solution)/shard_map/all_to_all | solution.py:97
  124.7 9.8 %all-to-all-start.2 = ((f32[8,1,128]{2,1,0:T(1,128)}), f32[8,1,128]{2,1,0:T(1,128)S(1)}, u32[]{:S(2)}, u32[]{:S(2)}) async-start(f32[8,1,128]{2,1,0:T(1,128)} %broadcast_in_dim.77), calls=%async_computation.2 | async-start | bytes 8192 | tf_op jit(solution)/shard_map/all_to_all | solution.py:97
  134.4 0.6 iota_compare_fusion.1
  135.2 0.7 gather_fusion.1
  135.9 0.7 gather_fusion.2
  136.6 2.4 %all-to-all-done.2 = f32[8,1,128]{2,1,0:T(1,128)S(1)} async-done(((f32[8,1,128]{2,1,0:T(1,128)}), f32[8,1,128]{2,1,0:T(1,128)S(1)}, u32[]{:S(2)}, u32[]{:S(2)}) %all-to-all-start.2) | async-done | bytes 4128 | tf_op jit(solution)/shard_map/all_to_all | solution.py:97
  139.1 0.7 multiply_subtract_fusion
  139.8 0.7 fusion.5
  (68 shorter events, 3.0 us)
Async XLA Ops:
  0.7 3.1 %copy-start = (f32[2,6656]{1,0:T(2,128)S(1)}, f32[2,6656]{1,0:T(2,128)}, u32[]{:S(2)}) copy-start(f32[2,6656]{1,0:T(2,128)} %param.6) | copy-start | bytes 159748
  0.7 3.1 %copy-start.2 = (f32[2,6656]{1,0:T(2,128)S(1)}, f32[2,6656]{1,0:T(2,128)}, u32[]{:S(2)}) copy-start(f32[2,6656]{1,0:T(2,128)} %param.7) | copy-start | bytes 159748
  4.0 14.5 %collective-permute-start.2 = (f32[108,8,128]{2,1,0:T(8,128)S(1)}, f32[108,8,128]{2,1,0:T(8,128)S(1)}, u32[]{:S(2)}, u32[]{:S(2)}) collective-permute-start(f32[108,8,128]{2,1,0:T(8,128)S(1)} %pad_maximum_fusion.3), channel_id=1, source_target_pairs={{0,8},{8,16},{16,24},{24,0},{1,9},{9,17},{17,25},{25,1},{2,10},{10... | collective-permute-start | bytes 1327112 | tf_op jit(solution)/shard_map/ppermute | solution.py:36
  8.0 9.6 %collective-permute-start.3 = (f32[104,8,128]{2,1,0:T(8,128)}, f32[104,8,128]{2,1,0:T(8,128)S(1)}, u32[]{:S(2)}, u32[]{:S(2)}) collective-permute-start(f32[104,8,128]{2,1,0:T(8,128)} %bitcast.23), channel_id=1, source_target_pairs={{0,24},{8,0},{16,8},{24,16},{1,25},{9,1},{17,9},{25,17},{2,26},{10... | collective-permute-start | bytes 1277960 | tf_op jit(solution)/shard_map/ppermute | solution.py:37
  11.5 15.1 %collective-permute-start.1 = (f32[108,8,128]{2,1,0:T(8,128)S(1)}, f32[108,8,128]{2,1,0:T(8,128)S(1)}, u32[]{:S(2)}, u32[]{:S(2)}) collective-permute-start(f32[108,8,128]{2,1,0:T(8,128)S(1)} %pad_maximum_fusion.2), channel_id=1, source_target_pairs={{0,24},{8,0},{16,8},{24,16},{1,25},{9,1},{17,9},{25,17},{2,26},{10... | collective-permute-start | bytes 1327112 | tf_op jit(solution)/shard_map/ppermute | solution.py:40
  15.7 10.9 %collective-permute-start = (f32[108,8,128]{2,1,0:T(8,128)}, f32[108,8,128]{2,1,0:T(8,128)S(1)}, u32[]{:S(2)}, u32[]{:S(2)}) collective-permute-start(f32[108,8,128]{2,1,0:T(8,128)} %pad_maximum_fusion.1), channel_id=1, source_target_pairs={{0,8},{8,16},{16,24},{24,0},{1,9},{9,17},{17,25},{25,1},{2,10},{10... | collective-permute-start | bytes 1327112 | tf_op jit(solution)/shard_map/ppermute | solution.py:39
  18.5 17.5 %collective-permute-start.4 = (f32[108,8,128]{2,1,0:T(8,128)S(1)}, f32[108,8,128]{2,1,0:T(8,128)S(1)}, u32[]{:S(2)}, u32[]{:S(2)}) collective-permute-start(f32[108,8,128]{2,1,0:T(8,128)S(1)} %pad_maximum_fusion.4), channel_id=1, source_target_pairs={{0,8},{8,16},{16,24},{24,0},{1,9},{9,17},{17,25},{25,1},{2,10},{10... | collective-permute-start | bytes 1327112 | tf_op jit(solution)/shard_map/ppermute | solution.py:44
  24.6 11.4 %collective-permute-start.5 = (f32[104,8,128]{2,1,0:T(8,128)}, f32[104,8,128]{2,1,0:T(8,128)}, u32[]{:S(2)}, u32[]{:S(2)}) collective-permute-start(f32[104,8,128]{2,1,0:T(8,128)} %bitcast_add_fusion), channel_id=1, source_target_pairs={{0,24},{8,0},{16,8},{24,16},{1,25},{9,1},{17,9},{25,17},{2,26},{10... | collective-permute-start | bytes 1277960 | tf_op jit(solution)/shard_map/ppermute | solution.py:45
  37.4 33.5 %copy-start.4 = (s32[64]{0:T(128)S(1)}, s32[64]{0:T(128)}, u32[]{:S(2)}) copy-start(s32[64]{0:T(128)} %param.8) | copy-start | bytes 772
  37.4 33.5 %copy-start.5 = (s32[64]{0:T(128)S(1)}, s32[64]{0:T(128)}, u32[]{:S(2)}) copy-start(s32[64]{0:T(128)} %param.9) | copy-start | bytes 772
  37.6 25.9 %collective-permute-start.7 = (f32[56,8,128]{2,1,0:T(8,128)S(1)}, f32[56,8,128]{2,1,0:T(8,128)S(1)}, u32[]{:S(2)}, u32[]{:S(2)}) collective-permute-start(f32[56,8,128]{2,1,0:T(8,128)S(1)} %pad_maximum_fusion.6), channel_id=1, source_target_pairs={{0,480},{32,0},{64,32},{96,64},{128,96},{160,128},{192,160},{224,1... | collective-permute-start | bytes 688136 | tf_op jit(solution)/shard_map/ppermute | solution.py:62
  51.4 12.1 %collective-permute-start.6 = (f32[56,8,128]{2,1,0:T(8,128)S(1)}, f32[56,8,128]{2,1,0:T(8,128)S(1)}, u32[]{:S(2)}, u32[]{:S(2)}) collective-permute-start(f32[56,8,128]{2,1,0:T(8,128)S(1)} %pad_maximum_fusion.5), channel_id=1, source_target_pairs={{0,32},{32,64},{64,96},{96,128},{128,160},{160,192},{192,224},{224... | collective-permute-start | bytes 688136 | tf_op jit(solution)/shard_map/ppermute | solution.py:61
  53.4 10.2 %collective-permute-start.8 = (f32[30,8,128]{2,1,0:T(8,128)S(1)}, f32[30,8,128]{2,1,0:T(8,128)S(1)}, u32[]{:S(2)}, u32[]{:S(2)}) collective-permute-start(f32[30,8,128]{2,1,0:T(8,128)S(1)} %pad_maximum_fusion.7), channel_id=1, source_target_pairs={{0,64},{32,96},{64,128},{96,160},{128,192},{160,224},{192,256},{22... | collective-permute-start | bytes 368648 | tf_op jit(solution)/shard_map/ppermute | solution.py:59
  55.3 8.2 %collective-permute-start.9 = (f32[26,8,128]{2,1,0:T(8,128)S(1)}, f32[26,8,128]{2,1,0:T(8,128)S(1)}, u32[]{:S(2)}, u32[]{:S(2)}) collective-permute-start(f32[26,8,128]{2,1,0:T(8,128)S(1)} %get-tuple-element.27), channel_id=1, source_target_pairs={{0,448},{32,480},{64,0},{96,32},{128,64},{160,96},{192,128},{224,1... | collective-permute-start | bytes 319496 | tf_op jit(solution)/shard_map/ppermute | solution.py:60
  64.3 22.6 %all-to-all-start = ((f32[4,17,8,128]{3,2,1,0:T(8,128)}), f32[4,17,8,128]{3,2,1,0:T(8,128)S(1)}, u32[]{:S(2)}, u32[]{:S(2)}) async-start(f32[4,17,8,128]{3,2,1,0:T(8,128)} %shard_map.76), calls=%async_computation | async-start | bytes 557056 | tf_op jit(solution)/shard_map/all_to_all | solution.py:164
  87.1 52.0 %copy-start.1 = (f32[2,6656]{1,0:T(2,128)S(1)}, f32[2,6656]{1,0:T(2,128)}, u32[]{:S(2)}) copy-start(f32[2,6656]{1,0:T(2,128)} %param.6) | copy-start | bytes 159748
  87.1 52.0 %copy-start.3 = (f32[2,6656]{1,0:T(2,128)S(1)}, f32[2,6656]{1,0:T(2,128)}, u32[]{:S(2)}) copy-start(f32[2,6656]{1,0:T(2,128)} %param.7) | copy-start | bytes 159748
  89.3 34.6 %all-to-all-start.1 = ((f32[192,4,128]{2,1,0:T(4,128)}), f32[192,4,128]{2,1,0:T(4,128)S(1)}, u32[]{:S(2)}, u32[]{:S(2)}) async-start(f32[192,4,128]{2,1,0:T(4,128)} %bitcast.44), calls=%async_computation.1 | async-start | bytes 786432 | tf_op jit(solution)/shard_map/all_to_all | solution.py:97
  124.7 14.3 %all-to-all-start.2 = ((f32[8,1,128]{2,1,0:T(1,128)}), f32[8,1,128]{2,1,0:T(1,128)S(1)}, u32[]{:S(2)}, u32[]{:S(2)}) async-start(f32[8,1,128]{2,1,0:T(1,128)} %broadcast_in_dim.77), calls=%async_computation.2 | async-start | bytes 8192 | tf_op jit(solution)/shard_map/all_to_all | solution.py:97

commit v4 on v3

--- a/solution.py
+++ b/solution.py
@@ -15,8 +15,10 @@
 
 NZ, NY, ROW_TILES, GROUPS, LANES = 16, 4, 16, 13, 128
 PER_ROW = NY * GROUPS
+TENSOR_SIZE = 8
+ENTRIES = 8 * ROW_TILES * PER_ROW * LANES * TENSOR_SIZE
 IN_VMEM = pl.BlockSpec(memory_space=pltpu.VMEM)
-ROWS_SENT, HELD_FROM, PART_AT = 12, 104, 232
+ROWS_SENT, HELD_FROM, PART_AT = 11, 104, 232
 
 
 def shift(n, by):
@@ -104,7 +106,6 @@
 def body(pseudo_grad, outer_params, momentum, save_pages, writer):
     z, y = lax.axis_index("z"), lax.axis_index("y")
     islands = NZ * NY
-    entries = pseudo_grad.shape[1] * pseudo_grad.shape[2] * lax.axis_size(TENSOR)
 
     order = jnp.arange(islands, dtype=jnp.int32)[:, None]
 
@@ -170,24 +171,51 @@
         compiler_params=pltpu.CompilerParams(vmem_limit_bytes=4 << 20),
     )(windows).reshape(-1, LANES)
 
-    outgoing = rows_of(table, send_index).reshape(-1, 4, LANES)
-    arrived = exchanged(outgoing, ISLAND).reshape(islands, 3, 4, LANES)
-    over_islands = jnp.sum(arrived[:, 2, 2], axis=0)
-    eight = exchanged(jnp.broadcast_to(over_islands, (lax.axis_size(TENSOR), 1, LANES)), TENSOR)
-    square_sum = jnp.sum(eight, axis=0)
-    scale = 1.0 / jnp.sqrt(square_sum / entries + epsilon)
-
-    mine = arrived[:, 2, :2].reshape(NZ, NY, 2, LANES)
-    mine = lax.dynamic_slice_in_dim(jnp.concatenate([mine, mine], axis=0), (GROUPS * z) % NZ, GROUPS, 0)
-    normed = (mine.transpose(2, 0, 1, 3) * scale).reshape(2, -1)
-    new_momentum = decay_rate * momentum + normed
-    new_master = outer_params - outer_rate * (normed + decay_rate * new_momentum)
-    arrived = arrived.reshape(-1, LANES)
+    outgoing = rows_of(table, send_index).reshape(-1, 1, LANES)
+    arrived = exchanged(outgoing, ISLAND).reshape(-1, LANES)
+    over_islands = pl.pallas_call(
+        part_kernel,
+        out_shape=jax.ShapeDtypeStruct((8, LANES), jnp.float32),
+        in_specs=[IN_VMEM],
+        out_specs=IN_VMEM,
+        compiler_params=pltpu.CompilerParams(vmem_limit_bytes=4 << 20),
+    )(arrived)
+    eight = exchanged(over_islands.reshape(lax.axis_size(TENSOR), -1, LANES), TENSOR).reshape(-1, LANES)
+
+    flat = jnp.arange(2 * PER_ROW, dtype=jnp.int32)
+    even, block = flat // PER_ROW, flat % PER_ROW
+    mine = rows_of(arrived, (((GROUPS * z + block // NY) % NZ) * NY + block % NY) * ROWS_SENT + 8 + even).reshape(2, -1)
     gradient_pages = rows_of(arrived, source * ROWS_SENT + slot)
     settled_pages = rows_of(arrived, source * ROWS_SENT + 4 + slot)
-    pages = settled_pages - (outer_rate * (1.0 + decay_rate)) * (gradient_pages * scale)
-    packed = jnp.where((place < own_length)[:, None], pages, 0.0).astype(jnp.bfloat16)
+    new_master, new_momentum, packed = pl.pallas_call(
+        final_kernel,
+        out_shape=(
+            jax.ShapeDtypeStruct(mine.shape, jnp.float32),
+            jax.ShapeDtypeStruct(mine.shape, jnp.float32),
+            jax.ShapeDtypeStruct(gradient_pages.shape, jnp.bfloat16),
+        ),
+        in_specs=[pl.BlockSpec(memory_space=pltpu.SMEM)] + [IN_VMEM] * 6,
+        out_specs=(IN_VMEM, IN_VMEM, IN_VMEM),
+        compiler_params=pltpu.CompilerParams(vmem_limit_bytes=4 << 20),
+    )(own_length, eight, mine, outer_params, momentum, gradient_pages, settled_pages)
     return (new_master, new_momentum, packed[None])
+
+
+def part_kernel(arrived, out):
+    parts = arrived[pl.ds(10, NZ * NY, stride=ROWS_SENT), :]
+    out[...] = jnp.broadcast_to(jnp.sum(parts, axis=0, keepdims=True), out.shape)
+
+
+def final_kernel(length, eight, mine, params, momentum, gradient_pages, settled_pages, master_out, momentum_out, pages_out):
+    square_sum = jnp.sum(eight[...], axis=0, keepdims=True) / (eight.shape[0] // TENSOR_SIZE)
+    scale = 1.0 / jnp.sqrt(square_sum / ENTRIES + epsilon)
+    normed = mine[...] * scale[:, :1]
+    new_momentum = decay_rate * momentum[...] + normed
+    momentum_out[...] = new_momentum
+    master_out[...] = params[...] - outer_rate * (normed + decay_rate * new_momentum)
+    pages = settled_pages[...] - (outer_rate * (1.0 + decay_rate)) * (gradient_pages[...] * scale)
+    place = lax.broadcasted_iota(jnp.int32, pages.shape, 0)
+    pages_out[...] = jnp.where(place < length[0], pages, 0.0).astype(jnp.bfloat16)
 
 
 def solution(mesh):

time: 141 us -> 140 us (level)
  other arithmetic: 8.44 us -> 6.34 us
  Pallas kernels: 0.91 us -> 2.87 us
  waiting for transfers between devices: 50.4 us -> 48.9 us
    pallas_call x0 -> x2, Pallas kernels: none -> 1.97 us  [the longest x1 1.36 us: body(): pl.pallas_call(final_kernel, out_shape=(jax.ShapeDtypeStruct(mine.shape,...]
    all_to_all x2, waiting for transfers between devices: 22.9 us -> 21.3 us  [exchanged(): return lax.all_to_all(array, axes, 0, 0, tiled=True)]
    gather x3 -> x4, local copies, waits for them, and re-layouts: 3.68 us -> 4.31 us  [rows_of(): return array.at[index].get(mode='promise_in_bounds')]
where the time goes in v4:
time: 140 us; the launch traced here: 139 us
  starting transfers between devices  72 us (51%)
  waiting for transfers between devices  48.9 us (35%)
  local copies, waits for them, and re-layouts  7.86 us (6%)
  other arithmetic  6.34 us (5%)
  Pallas kernels  2.87 us (2%)
    all_to_all x2, starting transfers between devices, exchanged(): return lax.all_to_all(array, axes, 0, 0, tiled=True)  21.6 us
    all_to_all x2, waiting for transfers between devices, exchanged(): return lax.all_to_all(array, axes, 0, 0, tiled=True)  21.3 us
    all_to_all x1, waiting for transfers between devices, body(): lax.all_to_all(windows, 'z', 0, 0, tiled=True, axis_index_groups=far)  15.4 us
    ppermute x1, starting transfers between devices, summed_in_window(): lax.ppermute(join(pick(classes, here + 3, 4), pick(riders, here + 3, 4)),...  13.8 us
    ppermute x1, waiting for transfers between devices, summed_around(): joined_down = lax.ppermute(for_below, axis, down)  9.36 us
    all_to_all x1, starting transfers between devices, body(): lax.all_to_all(windows, 'z', 0, 0, tiled=True, axis_index_groups=far)  6.62 us
    ppermute x1, starting transfers between devices, summed_around(): joined_up = lax.ppermute(for_above, axis, up)  6.04 us
    ppermute x1, starting transfers between devices, summed_in_window(): far_down = lax.ppermute(far[half:], axis, shift(n, -2))  5.47 us
  transfers between devices with their start and end apart: 13, of which 5 were waited for; matrix products, arithmetic and copies ran while one was open for 5% of the time, Pallas kernels for 0%

profile of v4, /device:TPU:1, one launch (start us, length us, event | category | flops | bytes accessed | tf_op | source)
XLA Modules:
  0.0 139.1 jit_solution(2816779375046277280)
XLA Ops:
  0.7 2.2 %dynamic-slice_bitcast_fusion = (f32[16,13,8,128]{3,2,1,0:T(8,128)S(1)}, f32[16,13,8,128]{3,2,1,0:T(8,128)S(1)}, f32[16,13,8,128]{3,2,1,0:T(8,128)S(1)}, f32[16,8,13,1,128]{4,1,3,2,0:T(8,128)S(1)}) fusion(f32[16,8,13,4,128]{4,1,3,2,0:T(8,128)} %bitcast.93, s32[]{:T(128)S(6)} %select_n.797, s32[]{:T(128)S(6)} %select_n.795, s32[]{:T(128)S(6)} %select_n.793, ...), kind=kLoop, calls=%fused_computation.5 | loop fusion | bytes 6815760 | tf_op jit(solution)/shard_map/transpose | solution.py:157
  2.9 0.8 fusion.45
  4.0 4.0 %collective-permute-start.2 = (f32[108,8,128]{2,1,0:T(8,128)S(1)}, f32[108,8,128]{2,1,0:T(8,128)S(1)}, u32[]{:S(2)}, u32[]{:S(2)}) collective-permute-start(f32[108,8,128]{2,1,0:T(8,128)S(1)} %pad_maximum_fusion.3), channel_id=1, source_target_pairs={{0,8},{8,16},{16,24},{24,0},{1,9},{9,17},{17,25},{25,1},{2,10},{10... | collective-permute-start | bytes 1327112 | tf_op jit(solution)/shard_map/ppermute | solution.py:38
  8.0 3.4 %collective-permute-start.3 = (f32[104,8,128]{2,1,0:T(8,128)}, f32[104,8,128]{2,1,0:T(8,128)S(1)}, u32[]{:S(2)}, u32[]{:S(2)}) collective-permute-start(f32[104,8,128]{2,1,0:T(8,128)} %bitcast.24), channel_id=1, source_target_pairs={{0,24},{8,0},{16,8},{24,16},{1,25},{9,1},{17,9},{25,17},{2,26},{10... | collective-permute-start | bytes 1277960 | tf_op jit(solution)/shard_map/ppermute | solution.py:39
  11.5 3.4 %collective-permute-start.1 = (f32[108,8,128]{2,1,0:T(8,128)S(1)}, f32[108,8,128]{2,1,0:T(8,128)S(1)}, u32[]{:S(2)}, u32[]{:S(2)}) collective-permute-start(f32[108,8,128]{2,1,0:T(8,128)S(1)} %pad_maximum_fusion.2), channel_id=1, source_target_pairs={{0,24},{8,0},{16,8},{24,16},{1,25},{9,1},{17,9},{25,17},{2,26},{10... | collective-permute-start | bytes 1327112 | tf_op jit(solution)/shard_map/ppermute | solution.py:42
  14.9 0.8 pad_maximum_fusion.1
  15.7 1.9 %collective-permute-start = (f32[108,8,128]{2,1,0:T(8,128)}, f32[108,8,128]{2,1,0:T(8,128)S(1)}, u32[]{:S(2)}, u32[]{:S(2)}) collective-permute-start(f32[108,8,128]{2,1,0:T(8,128)} %pad_maximum_fusion.1), channel_id=1, source_target_pairs={{0,8},{8,16},{16,24},{24,0},{1,9},{9,17},{17,25},{25,1},{2,10},{10... | collective-permute-start | bytes 1327112 | tf_op jit(solution)/shard_map/ppermute | solution.py:41
  17.7 0.8 bitcast_add_fusion
  18.6 6.0 %collective-permute-start.4 = (f32[108,8,128]{2,1,0:T(8,128)S(1)}, f32[108,8,128]{2,1,0:T(8,128)S(1)}, u32[]{:S(2)}, u32[]{:S(2)}) collective-permute-start(f32[108,8,128]{2,1,0:T(8,128)S(1)} %pad_maximum_fusion.4), channel_id=1, source_target_pairs={{0,8},{8,16},{16,24},{24,0},{1,9},{9,17},{17,25},{25,1},{2,10},{10... | collective-permute-start | bytes 1327112 | tf_op jit(solution)/shard_map/ppermute | solution.py:46
  24.6 1.9 %collective-permute-start.5 = (f32[104,8,128]{2,1,0:T(8,128)}, f32[104,8,128]{2,1,0:T(8,128)}, u32[]{:S(2)}, u32[]{:S(2)}) collective-permute-start(f32[104,8,128]{2,1,0:T(8,128)} %bitcast_add_fusion), channel_id=1, source_target_pairs={{0,24},{8,0},{16,8},{24,16},{1,25},{9,1},{17,9},{25,17},{2,26},{10... | collective-permute-start | bytes 1277960 | tf_op jit(solution)/shard_map/ppermute | solution.py:47
  26.7 9.4 %collective-permute-done.5 = f32[104,8,128]{2,1,0:T(8,128)} collective-permute-done((f32[104,8,128]{2,1,0:T(8,128)}, f32[104,8,128]{2,1,0:T(8,128)}, u32[]{:S(2)}, u32[]{:S(2)}) %collective-permute-start.5) | collective-permute-done | bytes 426016 | tf_op jit(solution)/shard_map/ppermute | solution.py:47
  36.2 1.2 slice_add_fusion.1
  37.7 13.8 %collective-permute-start.7 = (f32[56,8,128]{2,1,0:T(8,128)S(1)}, f32[56,8,128]{2,1,0:T(8,128)S(1)}, u32[]{:S(2)}, u32[]{:S(2)}) collective-permute-start(f32[56,8,128]{2,1,0:T(8,128)S(1)} %pad_maximum_fusion.6), channel_id=1, source_target_pairs={{0,480},{32,0},{64,32},{96,64},{128,96},{160,128},{192,160},{224,1... | collective-permute-start | bytes 688136 | tf_op jit(solution)/shard_map/ppermute | solution.py:64
  51.5 1.9 %collective-permute-start.6 = (f32[56,8,128]{2,1,0:T(8,128)S(1)}, f32[56,8,128]{2,1,0:T(8,128)S(1)}, u32[]{:S(2)}, u32[]{:S(2)}) collective-permute-start(f32[56,8,128]{2,1,0:T(8,128)S(1)} %pad_maximum_fusion.5), channel_id=1, source_target_pairs={{0,32},{32,64},{64,96},{96,128},{128,160},{160,192},{192,224},{224... | collective-permute-start | bytes 688136 | tf_op jit(solution)/shard_map/ppermute | solution.py:63
  53.4 1.9 %collective-permute-start.8 = (f32[30,8,128]{2,1,0:T(8,128)S(1)}, f32[30,8,128]{2,1,0:T(8,128)S(1)}, u32[]{:S(2)}, u32[]{:S(2)}) collective-permute-start(f32[30,8,128]{2,1,0:T(8,128)S(1)} %pad_maximum_fusion.7), channel_id=1, source_target_pairs={{0,64},{32,96},{64,128},{96,160},{128,192},{160,224},{192,256},{22... | collective-permute-start | bytes 368648 | tf_op jit(solution)/shard_map/ppermute | solution.py:61
  55.3 5.5 %collective-permute-start.9 = (f32[26,8,128]{2,1,0:T(8,128)S(1)}, f32[26,8,128]{2,1,0:T(8,128)S(1)}, u32[]{:S(2)}, u32[]{:S(2)}) collective-permute-start(f32[26,8,128]{2,1,0:T(8,128)S(1)} %get-tuple-element.31), channel_id=1, source_target_pairs={{0,448},{32,480},{64,0},{96,32},{128,64},{160,96},{192,128},{224,1... | collective-permute-start | bytes 319496 | tf_op jit(solution)/shard_map/ppermute | solution.py:62
  60.8 2.8 %collective-permute-done.9.far_down = f32[26,8,128]{2,1,0:T(8,128)S(1)} collective-permute-done((f32[26,8,128]{2,1,0:T(8,128)S(1)}, f32[26,8,128]{2,1,0:T(8,128)S(1)}, u32[]{:S(2)}, u32[]{:S(2)}) %collective-permute-start.9) | collective-permute-done | bytes 106528 | tf_op jit(solution)/shard_map/ppermute | solution.py:62
  63.6 0.8 shard_map.76
  64.4 6.6 %all-to-all-start = ((f32[4,17,8,128]{3,2,1,0:T(8,128)}), f32[4,17,8,128]{3,2,1,0:T(8,128)S(1)}, u32[]{:S(2)}, u32[]{:S(2)}) async-start(f32[4,17,8,128]{3,2,1,0:T(8,128)} %shard_map.76), calls=%async_computation | async-start | bytes 557056 | tf_op jit(solution)/shard_map/all_to_all | solution.py:165
  71.6 15.4 %all-to-all-done.windows = f32[4,17,8,128]{3,2,1,0:T(8,128)S(1)} async-done(((f32[4,17,8,128]{3,2,1,0:T(8,128)}), f32[4,17,8,128]{3,2,1,0:T(8,128)S(1)}, u32[]{:S(2)}, u32[]{:S(2)}) %all-to-all-start) | async-done | bytes 278560 | tf_op jit(solution)/shard_map/all_to_all | solution.py:165
  87.1 2.3 %gather_fusion = f32[704,128]{1,0:T(8,128)} fusion(f32[240,128]{1,0:T(8,128)S(1)} %bitcast.87, s32[1024]{0:T(1024)S(1)} %pad_clamp_fusion.3), kind=kCustom, calls=%fused_computation | custom fusion | bytes 723712 | tf_op jit(solution)/shard_map/gather | solution.py:103
  89.4 11.4 %all-to-all-start.1 = ((f32[704,1,128]{2,1,0:T(1,128)}), f32[704,1,128]{2,1,0:T(1,128)S(1)}, u32[]{:S(2)}, u32[]{:S(2)}) async-start(f32[704,1,128]{2,1,0:T(1,128)} %bitcast.46), calls=%async_computation.1 | async-start | bytes 720896 | tf_op jit(solution)/shard_map/all_to_all | solution.py:99
  100.9 0.6 fusion.39
  101.5 1.3 fusion.41
  102.8 0.7 compare_select_fusion.60
  103.6 18.9 %all-to-all-done.1 = f32[704,1,128]{2,1,0:T(1,128)S(1)} async-done(((f32[704,1,128]{2,1,0:T(1,128)}), f32[704,1,128]{2,1,0:T(1,128)S(1)}, u32[]{:S(2)}, u32[]{:S(2)}) %all-to-all-start.1) | async-done | bytes 360480 | tf_op jit(solution)/shard_map/all_to_all | solution.py:99
  123.1 10.2 %all-to-all-start.2 = ((f32[8,1,128]{2,1,0:T(1,128)}), f32[8,1,128]{2,1,0:T(1,128)S(1)}, u32[]{:S(2)}, u32[]{:S(2)}) async-start(f32[8,1,128]{2,1,0:T(1,128)} %bitcast.49), calls=%async_computation.2 | async-start | bytes 8192 | tf_op jit(solution)/shard_map/all_to_all | solution.py:99
  133.3 0.7 gather_fusion.2
  134.0 0.7 gather_fusion.3
  134.7 0.6 gather_fusion.1
  135.4 2.4 %all-to-all-done.2 = f32[8,1,128]{2,1,0:T(1,128)S(1)} async-done(((f32[8,1,128]{2,1,0:T(1,128)}), f32[8,1,128]{2,1,0:T(1,128)S(1)}, u32[]{:S(2)}, u32[]{:S(2)}) %all-to-all-start.2) | async-done | bytes 4128 | tf_op jit(solution)/shard_map/all_to_all | solution.py:99
  137.8 1.4 shard_map.79
  (59 shorter events, 2.2 us)
Async XLA Ops:
  0.7 3.1 %copy-start = (f32[2,6656]{1,0:T(2,128)S(1)}, f32[2,6656]{1,0:T(2,128)}, u32[]{:S(2)}) copy-start(f32[2,6656]{1,0:T(2,128)} %params.1) | copy-start | bytes 159748
  0.7 3.1 %copy-start.1 = (f32[2,6656]{1,0:T(2,128)S(1)}, f32[2,6656]{1,0:T(2,128)}, u32[]{:S(2)}) copy-start(f32[2,6656]{1,0:T(2,128)} %momentum.1) | copy-start | bytes 159748
  4.0 14.5 %collective-permute-start.2 = (f32[108,8,128]{2,1,0:T(8,128)S(1)}, f32[108,8,128]{2,1,0:T(8,128)S(1)}, u32[]{:S(2)}, u32[]{:S(2)}) collective-permute-start(f32[108,8,128]{2,1,0:T(8,128)S(1)} %pad_maximum_fusion.3), channel_id=1, source_target_pairs={{0,8},{8,16},{16,24},{24,0},{1,9},{9,17},{17,25},{25,1},{2,10},{10... | collective-permute-start | bytes 1327112 | tf_op jit(solution)/shard_map/ppermute | solution.py:38
  8.0 9.6 %collective-permute-start.3 = (f32[104,8,128]{2,1,0:T(8,128)}, f32[104,8,128]{2,1,0:T(8,128)S(1)}, u32[]{:S(2)}, u32[]{:S(2)}) collective-permute-start(f32[104,8,128]{2,1,0:T(8,128)} %bitcast.24), channel_id=1, source_target_pairs={{0,24},{8,0},{16,8},{24,16},{1,25},{9,1},{17,9},{25,17},{2,26},{10... | collective-permute-start | bytes 1277960 | tf_op jit(solution)/shard_map/ppermute | solution.py:39
  11.5 15.1 %collective-permute-start.1 = (f32[108,8,128]{2,1,0:T(8,128)S(1)}, f32[108,8,128]{2,1,0:T(8,128)S(1)}, u32[]{:S(2)}, u32[]{:S(2)}) collective-permute-start(f32[108,8,128]{2,1,0:T(8,128)S(1)} %pad_maximum_fusion.2), channel_id=1, source_target_pairs={{0,24},{8,0},{16,8},{24,16},{1,25},{9,1},{17,9},{25,17},{2,26},{10... | collective-permute-start | bytes 1327112 | tf_op jit(solution)/shard_map/ppermute | solution.py:42
  15.7 10.9 %collective-permute-start = (f32[108,8,128]{2,1,0:T(8,128)}, f32[108,8,128]{2,1,0:T(8,128)S(1)}, u32[]{:S(2)}, u32[]{:S(2)}) collective-permute-start(f32[108,8,128]{2,1,0:T(8,128)} %pad_maximum_fusion.1), channel_id=1, source_target_pairs={{0,8},{8,16},{16,24},{24,0},{1,9},{9,17},{17,25},{25,1},{2,10},{10... | collective-permute-start | bytes 1327112 | tf_op jit(solution)/shard_map/ppermute | solution.py:41
  18.6 17.5 %collective-permute-start.4 = (f32[108,8,128]{2,1,0:T(8,128)S(1)}, f32[108,8,128]{2,1,0:T(8,128)S(1)}, u32[]{:S(2)}, u32[]{:S(2)}) collective-permute-start(f32[108,8,128]{2,1,0:T(8,128)S(1)} %pad_maximum_fusion.4), channel_id=1, source_target_pairs={{0,8},{8,16},{16,24},{24,0},{1,9},{9,17},{17,25},{25,1},{2,10},{10... | collective-permute-start | bytes 1327112 | tf_op jit(solution)/shard_map/ppermute | solution.py:46
  24.6 11.4 %collective-permute-start.5 = (f32[104,8,128]{2,1,0:T(8,128)}, f32[104,8,128]{2,1,0:T(8,128)}, u32[]{:S(2)}, u32[]{:S(2)}) collective-permute-start(f32[104,8,128]{2,1,0:T(8,128)} %bitcast_add_fusion), channel_id=1, source_target_pairs={{0,24},{8,0},{16,8},{24,16},{1,25},{9,1},{17,9},{25,17},{2,26},{10... | collective-permute-start | bytes 1277960 | tf_op jit(solution)/shard_map/ppermute | solution.py:47
  37.4 33.6 %copy-start.2 = (s32[64]{0:T(128)S(1)}, s32[64]{0:T(128)}, u32[]{:S(2)}) copy-start(s32[64]{0:T(128)} %param.8) | copy-start | bytes 772
  37.5 33.6 %copy-start.3 = (s32[64]{0:T(128)S(1)}, s32[64]{0:T(128)}, u32[]{:S(2)}) copy-start(s32[64]{0:T(128)} %param.9) | copy-start | bytes 772
  37.7 25.9 %collective-permute-start.7 = (f32[56,8,128]{2,1,0:T(8,128)S(1)}, f32[56,8,128]{2,1,0:T(8,128)S(1)}, u32[]{:S(2)}, u32[]{:S(2)}) collective-permute-start(f32[56,8,128]{2,1,0:T(8,128)S(1)} %pad_maximum_fusion.6), channel_id=1, source_target_pairs={{0,480},{32,0},{64,32},{96,64},{128,96},{160,128},{192,160},{224,1... | collective-permute-start | bytes 688136 | tf_op jit(solution)/shard_map/ppermute | solution.py:64
  51.5 12.1 %collective-permute-start.6 = (f32[56,8,128]{2,1,0:T(8,128)S(1)}, f32[56,8,128]{2,1,0:T(8,128)S(1)}, u32[]{:S(2)}, u32[]{:S(2)}) collective-permute-start(f32[56,8,128]{2,1,0:T(8,128)S(1)} %pad_maximum_fusion.5), channel_id=1, source_target_pairs={{0,32},{32,64},{64,96},{96,128},{128,160},{160,192},{192,224},{224... | collective-permute-start | bytes 688136 | tf_op jit(solution)/shard_map/ppermute | solution.py:63
  53.4 10.2 %collective-permute-start.8 = (f32[30,8,128]{2,1,0:T(8,128)S(1)}, f32[30,8,128]{2,1,0:T(8,128)S(1)}, u32[]{:S(2)}, u32[]{:S(2)}) collective-permute-start(f32[30,8,128]{2,1,0:T(8,128)S(1)} %pad_maximum_fusion.7), channel_id=1, source_target_pairs={{0,64},{32,96},{64,128},{96,160},{128,192},{160,224},{192,256},{22... | collective-permute-start | bytes 368648 | tf_op jit(solution)/shard_map/ppermute | solution.py:61
  55.3 8.2 %collective-permute-start.9 = (f32[26,8,128]{2,1,0:T(8,128)S(1)}, f32[26,8,128]{2,1,0:T(8,128)S(1)}, u32[]{:S(2)}, u32[]{:S(2)}) collective-permute-start(f32[26,8,128]{2,1,0:T(8,128)S(1)} %get-tuple-element.31), channel_id=1, source_target_pairs={{0,448},{32,480},{64,0},{96,32},{128,64},{160,96},{192,128},{224,1... | collective-permute-start | bytes 319496 | tf_op jit(solution)/shard_map/ppermute | solution.py:62
  64.4 22.6 %all-to-all-start = ((f32[4,17,8,128]{3,2,1,0:T(8,128)}), f32[4,17,8,128]{3,2,1,0:T(8,128)S(1)}, u32[]{:S(2)}, u32[]{:S(2)}) async-start(f32[4,17,8,128]{3,2,1,0:T(8,128)} %shard_map.76), calls=%async_computation | async-start | bytes 557056 | tf_op jit(solution)/shard_map/all_to_all | solution.py:165
  89.4 33.1 %all-to-all-start.1 = ((f32[704,1,128]{2,1,0:T(1,128)}), f32[704,1,128]{2,1,0:T(1,128)S(1)}, u32[]{:S(2)}, u32[]{:S(2)}) async-start(f32[704,1,128]{2,1,0:T(1,128)} %bitcast.46), calls=%async_computation.1 | async-start | bytes 720896 | tf_op jit(solution)/shard_map/all_to_all | solution.py:99
  123.1 14.7 %all-to-all-start.2 = ((f32[8,1,128]{2,1,0:T(1,128)}), f32[8,1,128]{2,1,0:T(1,128)S(1)}, u32[]{:S(2)}, u32[]{:S(2)}) async-start(f32[8,1,128]{2,1,0:T(1,128)} %bitcast.49), calls=%async_computation.2 | async-start | bytes 8192 | tf_op jit(solution)/shard_map/all_to_all | solution.py:99

commit v5 on v4

--- a/solution.py
+++ b/solution.py
@@ -82,12 +82,18 @@
         out[chunk, GROUPS + 3] = far_up[2 * GROUPS + chunk]
 
 
-def table_kernel(windows, out):
+def outgoing_kernel(windows, chosen, out):
     mean = (windows[0, :GROUPS] + windows[1, :GROUPS] + windows[2, :GROUPS] + windows[3, :GROUPS]) / (NZ * NY)
-    out[:GROUPS] = mean
-    for chunk in range(4):
-        out[pl.ds(GROUPS + 4 * chunk, 4)] = windows[chunk, GROUPS:]
-    out[GROUPS + 16] = jnp.full((8, LANES), jnp.sum(mean * mean), jnp.float32)
+    part = jnp.full((1, 8, LANES), jnp.sum(mean * mean), jnp.float32)
+    held = [windows[chunk, GROUPS:] for chunk in range(4)]
+    rest = jnp.concatenate([mean, *held, part, jnp.zeros((2, 8, LANES), jnp.float32)], axis=0).reshape(256, LANES)
+    total = None
+    for _ in range(3):
+        piece = rest.astype(jnp.bfloat16)
+        rest = rest - piece.astype(jnp.float32)
+        rows = jnp.dot(chosen[...], piece, preferred_element_type=jnp.float32)
+        total = rows if total is None else total + rows
+    out[...] = total
 
 
 def rolled(array, by):
@@ -163,16 +169,16 @@
     windows = summed_in_window(classes.reshape(4, 4 * GROUPS, 8, LANES), settled, "z", NZ)
     far = [[4 * h + l for h in range(4)] for l in range(4)]
     windows = lax.all_to_all(windows, "z", 0, 0, tiled=True, axis_index_groups=far)
-    table = pl.pallas_call(
-        table_kernel,
-        out_shape=jax.ShapeDtypeStruct((GROUPS + 17, 8, LANES), jnp.float32),
-        in_specs=[IN_VMEM],
+    chosen = (send_index[:, None] == jnp.arange(256, dtype=jnp.int32)[None, :]).astype(jnp.bfloat16)
+
+    outgoing = pl.pallas_call(
+        outgoing_kernel,
+        out_shape=jax.ShapeDtypeStruct((ROWS_SENT * islands, LANES), jnp.float32),
+        in_specs=[IN_VMEM] * 2,
         out_specs=IN_VMEM,
-        compiler_params=pltpu.CompilerParams(vmem_limit_bytes=4 << 20),
-    )(windows).reshape(-1, LANES)
-
-    outgoing = rows_of(table, send_index).reshape(-1, 1, LANES)
-    arrived = exchanged(outgoing, ISLAND).reshape(-1, LANES)
+        compiler_params=pltpu.CompilerParams(vmem_limit_bytes=6 << 20),
+    )(windows, chosen)
+    arrived = exchanged(outgoing.reshape(-1, 1, LANES), ISLAND).reshape(-1, LANES)
     over_islands = pl.pallas_call(
         part_kernel,
         out_shape=jax.ShapeDtypeStruct((8, LANES), jnp.float32),

time: 140 us -> 139 us (level)
  local copies, waits for them, and re-layouts: 7.86 us -> 5.59 us
    gather x4 -> x3, local copies, waits for them, and re-layouts: 4.31 us -> 2.04 us  [rows_of(): return array.at[index].get(mode='promise_in_bounds')]
where the time goes in v5:
time: 139 us; the launch traced here: 138 us
  starting transfers between devices  72 us (52%)
  waiting for transfers between devices  48.9 us (35%)
  other arithmetic  6.26 us (5%)
  local copies, waits for them, and re-layouts  5.59 us (4%)
  Pallas kernels  4.08 us (3%)
    all_to_all x2, starting transfers between devices, exchanged(): return lax.all_to_all(array, axes, 0, 0, tiled=True)  21.6 us
    all_to_all x2, waiting for transfers between devices, exchanged(): return lax.all_to_all(array, axes, 0, 0, tiled=True)  21.3 us
    all_to_all x1, waiting for transfers between devices, body(): lax.all_to_all(windows, 'z', 0, 0, tiled=True, axis_index_groups=far)  15.5 us
    ppermute x1, starting transfers between devices, summed_in_window(): lax.ppermute(join(pick(classes, here + 3, 4), pick(riders, here + 3, 4)),...  13.7 us
    ppermute x1, waiting for transfers between devices, summed_around(): joined_down = lax.ppermute(for_below, axis, down)  9.36 us
    all_to_all x1, starting transfers between devices, body(): lax.all_to_all(windows, 'z', 0, 0, tiled=True, axis_index_groups=far)  6.62 us
    ppermute x1, starting transfers between devices, summed_around(): joined_up = lax.ppermute(for_above, axis, up)  6.05 us
    ppermute x1, starting transfers between devices, summed_in_window(): far_down = lax.ppermute(far[half:], axis, shift(n, -2))  5.47 us
  transfers between devices with their start and end apart: 13, of which 5 were waited for; matrix products, arithmetic and copies ran while one was open for 5% of the time, Pallas kernels for 0%

profile of v5, /device:TPU:1, one launch (start us, length us, event | category | flops | bytes accessed | tf_op | source)
XLA Modules:
  0.0 138.1 jit_solution(11895810854605043674)
XLA Ops:
  0.7 2.2 %dynamic-slice_bitcast_fusion = (f32[16,13,8,128]{3,2,1,0:T(8,128)S(1)}, f32[16,13,8,128]{3,2,1,0:T(8,128)S(1)}, f32[16,13,8,128]{3,2,1,0:T(8,128)S(1)}, f32[16,8,13,1,128]{4,1,3,2,0:T(8,128)S(1)}) fusion(f32[16,8,13,4,128]{4,1,3,2,0:T(8,128)} %bitcast.91, s32[]{:T(128)S(6)} %select_n.667, s32[]{:T(128)S(6)} %select_n.665, s32[]{:T(128)S(6)} %select_n.663, ...), kind=kLoop, calls=%fused_computation.4 | loop fusion | bytes 6815760 | tf_op jit(solution)/shard_map/transpose | solution.py:163
  2.9 0.8 fusion.80
  4.0 4.0 %collective-permute-start.2 = (f32[108,8,128]{2,1,0:T(8,128)S(1)}, f32[108,8,128]{2,1,0:T(8,128)S(1)}, u32[]{:S(2)}, u32[]{:S(2)}) collective-permute-start(f32[108,8,128]{2,1,0:T(8,128)S(1)} %pad_maximum_fusion.3), channel_id=1, source_target_pairs={{0,8},{8,16},{16,24},{24,0},{1,9},{9,17},{17,25},{25,1},{2,10},{10... | collective-permute-start | bytes 1327112 | tf_op jit(solution)/shard_map/ppermute | solution.py:38
  8.0 3.4 %collective-permute-start.3 = (f32[104,8,128]{2,1,0:T(8,128)}, f32[104,8,128]{2,1,0:T(8,128)S(1)}, u32[]{:S(2)}, u32[]{:S(2)}) collective-permute-start(f32[104,8,128]{2,1,0:T(8,128)} %bitcast.24), channel_id=1, source_target_pairs={{0,24},{8,0},{16,8},{24,16},{1,25},{9,1},{17,9},{25,17},{2,26},{10... | collective-permute-start | bytes 1277960 | tf_op jit(solution)/shard_map/ppermute | solution.py:39
  11.5 3.4 %collective-permute-start.1 = (f32[108,8,128]{2,1,0:T(8,128)S(1)}, f32[108,8,128]{2,1,0:T(8,128)S(1)}, u32[]{:S(2)}, u32[]{:S(2)}) collective-permute-start(f32[108,8,128]{2,1,0:T(8,128)S(1)} %pad_maximum_fusion.2), channel_id=1, source_target_pairs={{0,24},{8,0},{16,8},{24,16},{1,25},{9,1},{17,9},{25,17},{2,26},{10... | collective-permute-start | bytes 1327112 | tf_op jit(solution)/shard_map/ppermute | solution.py:42
  14.9 0.8 pad_maximum_fusion.1
  15.7 1.9 %collective-permute-start = (f32[108,8,128]{2,1,0:T(8,128)}, f32[108,8,128]{2,1,0:T(8,128)S(1)}, u32[]{:S(2)}, u32[]{:S(2)}) collective-permute-start(f32[108,8,128]{2,1,0:T(8,128)} %pad_maximum_fusion.1), channel_id=1, source_target_pairs={{0,8},{8,16},{16,24},{24,0},{1,9},{9,17},{17,25},{25,1},{2,10},{10... | collective-permute-start | bytes 1327112 | tf_op jit(solution)/shard_map/ppermute | solution.py:41
  17.7 0.8 bitcast_add_fusion
  18.6 6.0 %collective-permute-start.4 = (f32[108,8,128]{2,1,0:T(8,128)S(1)}, f32[108,8,128]{2,1,0:T(8,128)S(1)}, u32[]{:S(2)}, u32[]{:S(2)}) collective-permute-start(f32[108,8,128]{2,1,0:T(8,128)S(1)} %pad_maximum_fusion.4), channel_id=1, source_target_pairs={{0,8},{8,16},{16,24},{24,0},{1,9},{9,17},{17,25},{25,1},{2,10},{10... | collective-permute-start | bytes 1327112 | tf_op jit(solution)/shard_map/ppermute | solution.py:46
  24.6 1.9 %collective-permute-start.5 = (f32[104,8,128]{2,1,0:T(8,128)}, f32[104,8,128]{2,1,0:T(8,128)}, u32[]{:S(2)}, u32[]{:S(2)}) collective-permute-start(f32[104,8,128]{2,1,0:T(8,128)} %bitcast_add_fusion), channel_id=1, source_target_pairs={{0,24},{8,0},{16,8},{24,16},{1,25},{9,1},{17,9},{25,17},{2,26},{10... | collective-permute-start | bytes 1277960 | tf_op jit(solution)/shard_map/ppermute | solution.py:47
  26.7 9.4 %collective-permute-done.5 = f32[104,8,128]{2,1,0:T(8,128)} collective-permute-done((f32[104,8,128]{2,1,0:T(8,128)}, f32[104,8,128]{2,1,0:T(8,128)}, u32[]{:S(2)}, u32[]{:S(2)}) %collective-permute-start.5) | collective-permute-done | bytes 426016 | tf_op jit(solution)/shard_map/ppermute | solution.py:47
  36.2 1.2 slice_add_fusion.1
  37.7 13.7 %collective-permute-start.7 = (f32[56,8,128]{2,1,0:T(8,128)S(1)}, f32[56,8,128]{2,1,0:T(8,128)S(1)}, u32[]{:S(2)}, u32[]{:S(2)}) collective-permute-start(f32[56,8,128]{2,1,0:T(8,128)S(1)} %pad_maximum_fusion.6), channel_id=1, source_target_pairs={{0,480},{32,0},{64,32},{96,64},{128,96},{160,128},{192,160},{224,1... | collective-permute-start | bytes 688136 | tf_op jit(solution)/shard_map/ppermute | solution.py:64
  51.5 1.9 %collective-permute-start.6 = (f32[56,8,128]{2,1,0:T(8,128)S(1)}, f32[56,8,128]{2,1,0:T(8,128)S(1)}, u32[]{:S(2)}, u32[]{:S(2)}) collective-permute-start(f32[56,8,128]{2,1,0:T(8,128)S(1)} %pad_maximum_fusion.5), channel_id=1, source_target_pairs={{0,32},{32,64},{64,96},{96,128},{128,160},{160,192},{192,224},{224... | collective-permute-start | bytes 688136 | tf_op jit(solution)/shard_map/ppermute | solution.py:63
  53.4 1.9 %collective-permute-start.8 = (f32[30,8,128]{2,1,0:T(8,128)S(1)}, f32[30,8,128]{2,1,0:T(8,128)S(1)}, u32[]{:S(2)}, u32[]{:S(2)}) collective-permute-start(f32[30,8,128]{2,1,0:T(8,128)S(1)} %pad_maximum_fusion.7), channel_id=1, source_target_pairs={{0,64},{32,96},{64,128},{96,160},{128,192},{160,224},{192,256},{22... | collective-permute-start | bytes 368648 | tf_op jit(solution)/shard_map/ppermute | solution.py:61
  55.3 5.5 %collective-permute-start.9 = (f32[26,8,128]{2,1,0:T(8,128)S(1)}, f32[26,8,128]{2,1,0:T(8,128)S(1)}, u32[]{:S(2)}, u32[]{:S(2)}) collective-permute-start(f32[26,8,128]{2,1,0:T(8,128)S(1)} %get-tuple-element.31), channel_id=1, source_target_pairs={{0,448},{32,480},{64,0},{96,32},{128,64},{160,96},{192,128},{224,1... | collective-permute-start | bytes 319496 | tf_op jit(solution)/shard_map/ppermute | solution.py:62
  60.8 2.8 %collective-permute-done.9.far_down = f32[26,8,128]{2,1,0:T(8,128)S(1)} collective-permute-done((f32[26,8,128]{2,1,0:T(8,128)S(1)}, f32[26,8,128]{2,1,0:T(8,128)S(1)}, u32[]{:S(2)}, u32[]{:S(2)}) %collective-permute-start.9) | collective-permute-done | bytes 106528 | tf_op jit(solution)/shard_map/ppermute | solution.py:62
  63.6 0.8 shard_map.76
  64.4 6.6 %all-to-all-start = ((f32[4,17,8,128]{3,2,1,0:T(8,128)}), f32[4,17,8,128]{3,2,1,0:T(8,128)S(1)}, u32[]{:S(2)}, u32[]{:S(2)}) async-start(f32[4,17,8,128]{3,2,1,0:T(8,128)} %shard_map.76), calls=%async_computation | async-start | bytes 557056 | tf_op jit(solution)/shard_map/all_to_all | solution.py:171
  71.5 15.5 %all-to-all-done.windows = f32[4,17,8,128]{3,2,1,0:T(8,128)S(1)} async-done(((f32[4,17,8,128]{3,2,1,0:T(8,128)}), f32[4,17,8,128]{3,2,1,0:T(8,128)S(1)}, u32[]{:S(2)}, u32[]{:S(2)}) %all-to-all-start) | async-done | bytes 278560 | tf_op jit(solution)/shard_map/all_to_all | solution.py:171
  87.0 1.3 shard_map.77
  88.2 11.5 %all-to-all-start.1 = ((f32[704,1,128]{2,1,0:T(1,128)}), f32[704,1,128]{2,1,0:T(1,128)S(1)}, u32[]{:S(2)}, u32[]{:S(2)}) async-start(f32[704,1,128]{2,1,0:T(1,128)} %bitcast.45), calls=%async_computation.1 | async-start | bytes 720896 | tf_op jit(solution)/shard_map/all_to_all | solution.py:105
  99.7 0.6 fusion.74
  100.4 1.3 fusion.76
  101.7 0.7 compare_select_fusion.2
  102.4 18.9 %all-to-all-done.1 = f32[704,1,128]{2,1,0:T(1,128)S(1)} async-done(((f32[704,1,128]{2,1,0:T(1,128)}), f32[704,1,128]{2,1,0:T(1,128)S(1)}, u32[]{:S(2)}, u32[]{:S(2)}) %all-to-all-start.1) | async-done | bytes 360480 | tf_op jit(solution)/shard_map/all_to_all | solution.py:105
  121.9 10.2 %all-to-all-start.2 = ((f32[8,1,128]{2,1,0:T(1,128)}), f32[8,1,128]{2,1,0:T(1,128)S(1)}, u32[]{:S(2)}, u32[]{:S(2)}) async-start(f32[8,1,128]{2,1,0:T(1,128)} %bitcast.48), calls=%async_computation.2 | async-start | bytes 8192 | tf_op jit(solution)/shard_map/all_to_all | solution.py:105
  132.1 0.7 gather_fusion.1
  132.9 0.7 gather_fusion.2
  133.6 0.6 gather_fusion
  134.2 2.4 %all-to-all-done.2 = f32[8,1,128]{2,1,0:T(1,128)S(1)} async-done(((f32[8,1,128]{2,1,0:T(1,128)}), f32[8,1,128]{2,1,0:T(1,128)S(1)}, u32[]{:S(2)}, u32[]{:S(2)}) %all-to-all-start.2) | async-done | bytes 4128 | tf_op jit(solution)/shard_map/all_to_all | solution.py:105
  136.6 1.4 %shard_map.79 = (f32[2,6656]{1,0:T(2,128)}, f32[2,6656]{1,0:T(2,128)}, bf16[208,128]{1,0:T(8,128)(2,1)}) custom-call(s32[1]{0:T(128)} %bitcast.length, f32[8,128]{1,0:T(8,128)S(1)} %bitcast.90, f32[2,6656]{1,0:T(2,128)S(1)} %reshape.928.mine, f32[2,6656]{1,0:T(2,128)S(1)} %copy-done, f32[2,6656]{1,0:T(2,128)S(1)} %copy-done.1, f32[208,128]{1,0:T(8,128)S(1)} %gather_fusion.1, ...), custom_call_target="tpu_custom_call" | custom-call | tf_op jit(solution)/shard_map/pallas_call | solution.py:196
  (58 shorter events, 2.0 us)
Async XLA Ops:
  0.7 3.1 %copy-start = (f32[2,6656]{1,0:T(2,128)S(1)}, f32[2,6656]{1,0:T(2,128)}, u32[]{:S(2)}) copy-start(f32[2,6656]{1,0:T(2,128)} %params.1) | copy-start | bytes 159748
  0.7 3.1 %copy-start.1 = (f32[2,6656]{1,0:T(2,128)S(1)}, f32[2,6656]{1,0:T(2,128)}, u32[]{:S(2)}) copy-start(f32[2,6656]{1,0:T(2,128)} %momentum.1) | copy-start | bytes 159748
  4.0 14.5 %collective-permute-start.2 = (f32[108,8,128]{2,1,0:T(8,128)S(1)}, f32[108,8,128]{2,1,0:T(8,128)S(1)}, u32[]{:S(2)}, u32[]{:S(2)}) collective-permute-start(f32[108,8,128]{2,1,0:T(8,128)S(1)} %pad_maximum_fusion.3), channel_id=1, source_target_pairs={{0,8},{8,16},{16,24},{24,0},{1,9},{9,17},{17,25},{25,1},{2,10},{10... | collective-permute-start | bytes 1327112 | tf_op jit(solution)/shard_map/ppermute | solution.py:38
  8.0 9.6 %collective-permute-start.3 = (f32[104,8,128]{2,1,0:T(8,128)}, f32[104,8,128]{2,1,0:T(8,128)S(1)}, u32[]{:S(2)}, u32[]{:S(2)}) collective-permute-start(f32[104,8,128]{2,1,0:T(8,128)} %bitcast.24), channel_id=1, source_target_pairs={{0,24},{8,0},{16,8},{24,16},{1,25},{9,1},{17,9},{25,17},{2,26},{10... | collective-permute-start | bytes 1277960 | tf_op jit(solution)/shard_map/ppermute | solution.py:39
  11.5 15.1 %collective-permute-start.1 = (f32[108,8,128]{2,1,0:T(8,128)S(1)}, f32[108,8,128]{2,1,0:T(8,128)S(1)}, u32[]{:S(2)}, u32[]{:S(2)}) collective-permute-start(f32[108,8,128]{2,1,0:T(8,128)S(1)} %pad_maximum_fusion.2), channel_id=1, source_target_pairs={{0,24},{8,0},{16,8},{24,16},{1,25},{9,1},{17,9},{25,17},{2,26},{10... | collective-permute-start | bytes 1327112 | tf_op jit(solution)/shard_map/ppermute | solution.py:42
  15.7 10.9 %collective-permute-start = (f32[108,8,128]{2,1,0:T(8,128)}, f32[108,8,128]{2,1,0:T(8,128)S(1)}, u32[]{:S(2)}, u32[]{:S(2)}) collective-permute-start(f32[108,8,128]{2,1,0:T(8,128)} %pad_maximum_fusion.1), channel_id=1, source_target_pairs={{0,8},{8,16},{16,24},{24,0},{1,9},{9,17},{17,25},{25,1},{2,10},{10... | collective-permute-start | bytes 1327112 | tf_op jit(solution)/shard_map/ppermute | solution.py:41
  18.6 17.5 %collective-permute-start.4 = (f32[108,8,128]{2,1,0:T(8,128)S(1)}, f32[108,8,128]{2,1,0:T(8,128)S(1)}, u32[]{:S(2)}, u32[]{:S(2)}) collective-permute-start(f32[108,8,128]{2,1,0:T(8,128)S(1)} %pad_maximum_fusion.4), channel_id=1, source_target_pairs={{0,8},{8,16},{16,24},{24,0},{1,9},{9,17},{17,25},{25,1},{2,10},{10... | collective-permute-start | bytes 1327112 | tf_op jit(solution)/shard_map/ppermute | solution.py:46
  24.6 11.4 %collective-permute-start.5 = (f32[104,8,128]{2,1,0:T(8,128)}, f32[104,8,128]{2,1,0:T(8,128)}, u32[]{:S(2)}, u32[]{:S(2)}) collective-permute-start(f32[104,8,128]{2,1,0:T(8,128)} %bitcast_add_fusion), channel_id=1, source_target_pairs={{0,24},{8,0},{16,8},{24,16},{1,25},{9,1},{17,9},{25,17},{2,26},{10... | collective-permute-start | bytes 1277960 | tf_op jit(solution)/shard_map/ppermute | solution.py:47
  37.4 33.5 %copy-start.2 = (s32[64]{0:T(128)S(1)}, s32[64]{0:T(128)}, u32[]{:S(2)}) copy-start(s32[64]{0:T(128)} %param.8) | copy-start | bytes 772
  37.5 33.5 %copy-start.3 = (s32[64]{0:T(128)S(1)}, s32[64]{0:T(128)}, u32[]{:S(2)}) copy-start(s32[64]{0:T(128)} %param.9) | copy-start | bytes 772
  37.7 25.9 %collective-permute-start.7 = (f32[56,8,128]{2,1,0:T(8,128)S(1)}, f32[56,8,128]{2,1,0:T(8,128)S(1)}, u32[]{:S(2)}, u32[]{:S(2)}) collective-permute-start(f32[56,8,128]{2,1,0:T(8,128)S(1)} %pad_maximum_fusion.6), channel_id=1, source_target_pairs={{0,480},{32,0},{64,32},{96,64},{128,96},{160,128},{192,160},{224,1... | collective-permute-start | bytes 688136 | tf_op jit(solution)/shard_map/ppermute | solution.py:64
  51.5 12.1 %collective-permute-start.6 = (f32[56,8,128]{2,1,0:T(8,128)S(1)}, f32[56,8,128]{2,1,0:T(8,128)S(1)}, u32[]{:S(2)}, u32[]{:S(2)}) collective-permute-start(f32[56,8,128]{2,1,0:T(8,128)S(1)} %pad_maximum_fusion.5), channel_id=1, source_target_pairs={{0,32},{32,64},{64,96},{96,128},{128,160},{160,192},{192,224},{224... | collective-permute-start | bytes 688136 | tf_op jit(solution)/shard_map/ppermute | solution.py:63
  53.4 10.2 %collective-permute-start.8 = (f32[30,8,128]{2,1,0:T(8,128)S(1)}, f32[30,8,128]{2,1,0:T(8,128)S(1)}, u32[]{:S(2)}, u32[]{:S(2)}) collective-permute-start(f32[30,8,128]{2,1,0:T(8,128)S(1)} %pad_maximum_fusion.7), channel_id=1, source_target_pairs={{0,64},{32,96},{64,128},{96,160},{128,192},{160,224},{192,256},{22... | collective-permute-start | bytes 368648 | tf_op jit(solution)/shard_map/ppermute | solution.py:61
  55.3 8.2 %collective-permute-start.9 = (f32[26,8,128]{2,1,0:T(8,128)S(1)}, f32[26,8,128]{2,1,0:T(8,128)S(1)}, u32[]{:S(2)}, u32[]{:S(2)}) collective-permute-start(f32[26,8,128]{2,1,0:T(8,128)S(1)} %get-tuple-element.31), channel_id=1, source_target_pairs={{0,448},{32,480},{64,0},{96,32},{128,64},{160,96},{192,128},{224,1... | collective-permute-start | bytes 319496 | tf_op jit(solution)/shard_map/ppermute | solution.py:62
  64.4 22.6 %all-to-all-start = ((f32[4,17,8,128]{3,2,1,0:T(8,128)}), f32[4,17,8,128]{3,2,1,0:T(8,128)S(1)}, u32[]{:S(2)}, u32[]{:S(2)}) async-start(f32[4,17,8,128]{3,2,1,0:T(8,128)} %shard_map.76), calls=%async_computation | async-start | bytes 557056 | tf_op jit(solution)/shard_map/all_to_all | solution.py:171
  88.2 33.1 %all-to-all-start.1 = ((f32[704,1,128]{2,1,0:T(1,128)}), f32[704,1,128]{2,1,0:T(1,128)S(1)}, u32[]{:S(2)}, u32[]{:S(2)}) async-start(f32[704,1,128]{2,1,0:T(1,128)} %bitcast.45), calls=%async_computation.1 | async-start | bytes 720896 | tf_op jit(solution)/shard_map/all_to_all | solution.py:105
  121.9 14.7 %all-to-all-start.2 = ((f32[8,1,128]{2,1,0:T(1,128)}), f32[8,1,128]{2,1,0:T(1,128)S(1)}, u32[]{:S(2)}, u32[]{:S(2)}) async-start(f32[8,1,128]{2,1,0:T(1,128)} %bitcast.48), calls=%async_computation.2 | async-start | bytes 8192 | tf_op jit(solution)/shard_map/all_to_all | solution.py:105

commit v6 on v5

--- a/solution.py
+++ b/solution.py
@@ -139,12 +139,12 @@
 
     flat = jnp.arange(ROWS_SENT * islands, dtype=jnp.int32)
     target, kind = flat // ROWS_SENT, flat % ROWS_SENT
-    held_index, sum_index = page_for(target, kind % 4)
+    held_index, sum_index = page_for(target, (kind + 3) % 4)
     tile = GROUPS * (target // NY)
     group = (z - tile) % NZ
-    row_index = jnp.where(group < GROUPS, 8 * ((tile + group) // NZ), 0) + 2 * (target % NY) + kind % 2
-    send_index = jnp.where(kind < 4, sum_index, jnp.where(kind < 8, HELD_FROM + held_index, row_index))
-    send_index = jnp.where(kind < 10, send_index, PART_AT)
+    row_index = jnp.where(group < GROUPS, 8 * ((tile + group) // NZ), 0) + 2 * (target % NY) + (kind + 1) % 2
+    send_index = jnp.where(kind < 5, sum_index, jnp.where(kind < 9, HELD_FROM + held_index, row_index))
+    send_index = jnp.where(kind > 0, send_index, PART_AT)
     own_start, own_length = window_of((z * NY + y)[None])
     place = jnp.arange(208, dtype=jnp.int32)
     page = jnp.minimum(own_start + place, 6655)
@@ -190,9 +190,9 @@
 
     flat = jnp.arange(2 * PER_ROW, dtype=jnp.int32)
     even, block = flat // PER_ROW, flat % PER_ROW
-    mine = rows_of(arrived, (((GROUPS * z + block // NY) % NZ) * NY + block % NY) * ROWS_SENT + 8 + even).reshape(2, -1)
-    gradient_pages = rows_of(arrived, source * ROWS_SENT + slot)
-    settled_pages = rows_of(arrived, source * ROWS_SENT + 4 + slot)
+    mine = rows_of(arrived, (((GROUPS * z + block // NY) % NZ) * NY + block % NY) * ROWS_SENT + 9 + even).reshape(2, -1)
+    gradient_pages = rows_of(arrived, source * ROWS_SENT + 1 + slot)
+    settled_pages = rows_of(arrived, source * ROWS_SENT + 5 + slot)
     new_master, new_momentum, packed = pl.pallas_call(
         final_kernel,
         out_shape=(
@@ -208,7 +208,7 @@
 
 
 def part_kernel(arrived, out):
-    parts = arrived[pl.ds(10, NZ * NY, stride=ROWS_SENT), :]
+    parts = arrived[pl.ds(0, NZ * NY, stride=ROWS_SENT), :]
     out[...] = jnp.broadcast_to(jnp.sum(parts, axis=0, keepdims=True), out.shape)
 
 

time: 139 us -> 139 us (level)
  no operation moved by 1% of the time
where the time goes in v6:
time: 139 us; the launch traced here: 138 us
  starting transfers between devices  72 us (52%)
  waiting for transfers between devices  48.9 us (35%)
  other arithmetic  6.26 us (5%)
  local copies, waits for them, and re-layouts  5.59 us (4%)
  Pallas kernels  4.08 us (3%)
    all_to_all x2, starting transfers between devices, exchanged(): return lax.all_to_all(array, axes, 0, 0, tiled=True)  21.6 us
    all_to_all x2, waiting for transfers between devices, exchanged(): return lax.all_to_all(array, axes, 0, 0, tiled=True)  21.3 us
    all_to_all x1, waiting for transfers between devices, body(): lax.all_to_all(windows, 'z', 0, 0, tiled=True, axis_index_groups=far)  15.5 us
    ppermute x1, starting transfers between devices, summed_in_window(): lax.ppermute(join(pick(classes, here + 3, 4), pick(riders, here + 3, 4)),...  13.7 us
    ppermute x1, waiting for transfers between devices, summed_around(): joined_down = lax.ppermute(for_below, axis, down)  9.36 us
    all_to_all x1, starting transfers between devices, body(): lax.all_to_all(windows, 'z', 0, 0, tiled=True, axis_index_groups=far)  6.62 us
    ppermute x1, starting transfers between devices, summed_around(): joined_up = lax.ppermute(for_above, axis, up)  6.05 us
    ppermute x1, starting transfers between devices, summed_in_window(): far_down = lax.ppermute(far[half:], axis, shift(n, -2))  5.47 us
  transfers between devices with their start and end apart: 13, of which 5 were waited for; matrix products, arithmetic and copies ran while one was open for 5% of the time, Pallas kernels for 0%

profile of v6, /device:TPU:1, one launch (start us, length us, event | category | flops | bytes accessed | tf_op | source)
XLA Modules:
  0.0 138.1 jit_solution(7281771671784881412)
XLA Ops:
  0.7 2.2 %dynamic-slice_bitcast_fusion = (f32[16,13,8,128]{3,2,1,0:T(8,128)S(1)}, f32[16,13,8,128]{3,2,1,0:T(8,128)S(1)}, f32[16,13,8,128]{3,2,1,0:T(8,128)S(1)}, f32[16,8,13,1,128]{4,1,3,2,0:T(8,128)S(1)}) fusion(f32[16,8,13,4,128]{4,1,3,2,0:T(8,128)} %bitcast.91, s32[]{:T(128)S(6)} %select_n.667, s32[]{:T(128)S(6)} %select_n.665, s32[]{:T(128)S(6)} %select_n.663, ...), kind=kLoop, calls=%fused_computation.4 | loop fusion | bytes 6815760 | tf_op jit(solution)/shard_map/transpose | solution.py:163
  2.9 0.8 fusion.81
  4.0 4.0 %collective-permute-start.2 = (f32[108,8,128]{2,1,0:T(8,128)S(1)}, f32[108,8,128]{2,1,0:T(8,128)S(1)}, u32[]{:S(2)}, u32[]{:S(2)}) collective-permute-start(f32[108,8,128]{2,1,0:T(8,128)S(1)} %pad_maximum_fusion.3), channel_id=1, source_target_pairs={{0,8},{8,16},{16,24},{24,0},{1,9},{9,17},{17,25},{25,1},{2,10},{10... | collective-permute-start | bytes 1327112 | tf_op jit(solution)/shard_map/ppermute | solution.py:38
  8.0 3.4 %collective-permute-start.3 = (f32[104,8,128]{2,1,0:T(8,128)}, f32[104,8,128]{2,1,0:T(8,128)S(1)}, u32[]{:S(2)}, u32[]{:S(2)}) collective-permute-start(f32[104,8,128]{2,1,0:T(8,128)} %bitcast.24), channel_id=1, source_target_pairs={{0,24},{8,0},{16,8},{24,16},{1,25},{9,1},{17,9},{25,17},{2,26},{10... | collective-permute-start | bytes 1277960 | tf_op jit(solution)/shard_map/ppermute | solution.py:39
  11.5 3.4 %collective-permute-start.1 = (f32[108,8,128]{2,1,0:T(8,128)S(1)}, f32[108,8,128]{2,1,0:T(8,128)S(1)}, u32[]{:S(2)}, u32[]{:S(2)}) collective-permute-start(f32[108,8,128]{2,1,0:T(8,128)S(1)} %pad_maximum_fusion.2), channel_id=1, source_target_pairs={{0,24},{8,0},{16,8},{24,16},{1,25},{9,1},{17,9},{25,17},{2,26},{10... | collective-permute-start | bytes 1327112 | tf_op jit(solution)/shard_map/ppermute | solution.py:42
  14.9 0.8 pad_maximum_fusion.1
  15.7 1.9 %collective-permute-start = (f32[108,8,128]{2,1,0:T(8,128)}, f32[108,8,128]{2,1,0:T(8,128)S(1)}, u32[]{:S(2)}, u32[]{:S(2)}) collective-permute-start(f32[108,8,128]{2,1,0:T(8,128)} %pad_maximum_fusion.1), channel_id=1, source_target_pairs={{0,8},{8,16},{16,24},{24,0},{1,9},{9,17},{17,25},{25,1},{2,10},{10... | collective-permute-start | bytes 1327112 | tf_op jit(solution)/shard_map/ppermute | solution.py:41
  17.7 0.8 bitcast_add_fusion
  18.6 6.0 %collective-permute-start.4 = (f32[108,8,128]{2,1,0:T(8,128)S(1)}, f32[108,8,128]{2,1,0:T(8,128)S(1)}, u32[]{:S(2)}, u32[]{:S(2)}) collective-permute-start(f32[108,8,128]{2,1,0:T(8,128)S(1)} %pad_maximum_fusion.4), channel_id=1, source_target_pairs={{0,8},{8,16},{16,24},{24,0},{1,9},{9,17},{17,25},{25,1},{2,10},{10... | collective-permute-start | bytes 1327112 | tf_op jit(solution)/shard_map/ppermute | solution.py:46
  24.6 1.9 %collective-permute-start.5 = (f32[104,8,128]{2,1,0:T(8,128)}, f32[104,8,128]{2,1,0:T(8,128)}, u32[]{:S(2)}, u32[]{:S(2)}) collective-permute-start(f32[104,8,128]{2,1,0:T(8,128)} %bitcast_add_fusion), channel_id=1, source_target_pairs={{0,24},{8,0},{16,8},{24,16},{1,25},{9,1},{17,9},{25,17},{2,26},{10... | collective-permute-start | bytes 1277960 | tf_op jit(solution)/shard_map/ppermute | solution.py:47
  26.7 9.4 %collective-permute-done.5 = f32[104,8,128]{2,1,0:T(8,128)} collective-permute-done((f32[104,8,128]{2,1,0:T(8,128)}, f32[104,8,128]{2,1,0:T(8,128)}, u32[]{:S(2)}, u32[]{:S(2)}) %collective-permute-start.5) | collective-permute-done | bytes 426016 | tf_op jit(solution)/shard_map/ppermute | solution.py:47
  36.2 1.2 slice_add_fusion.1
  37.7 13.7 %collective-permute-start.7 = (f32[56,8,128]{2,1,0:T(8,128)S(1)}, f32[56,8,128]{2,1,0:T(8,128)S(1)}, u32[]{:S(2)}, u32[]{:S(2)}) collective-permute-start(f32[56,8,128]{2,1,0:T(8,128)S(1)} %pad_maximum_fusion.6), channel_id=1, source_target_pairs={{0,480},{32,0},{64,32},{96,64},{128,96},{160,128},{192,160},{224,1... | collective-permute-start | bytes 688136 | tf_op jit(solution)/shard_map/ppermute | solution.py:64
  51.5 1.9 %collective-permute-start.6 = (f32[56,8,128]{2,1,0:T(8,128)S(1)}, f32[56,8,128]{2,1,0:T(8,128)S(1)}, u32[]{:S(2)}, u32[]{:S(2)}) collective-permute-start(f32[56,8,128]{2,1,0:T(8,128)S(1)} %pad_maximum_fusion.5), channel_id=1, source_target_pairs={{0,32},{32,64},{64,96},{96,128},{128,160},{160,192},{192,224},{224... | collective-permute-start | bytes 688136 | tf_op jit(solution)/shard_map/ppermute | solution.py:63
  53.4 1.9 %collective-permute-start.8 = (f32[30,8,128]{2,1,0:T(8,128)S(1)}, f32[30,8,128]{2,1,0:T(8,128)S(1)}, u32[]{:S(2)}, u32[]{:S(2)}) collective-permute-start(f32[30,8,128]{2,1,0:T(8,128)S(1)} %pad_maximum_fusion.7), channel_id=1, source_target_pairs={{0,64},{32,96},{64,128},{96,160},{128,192},{160,224},{192,256},{22... | collective-permute-start | bytes 368648 | tf_op jit(solution)/shard_map/ppermute | solution.py:61
  55.3 5.5 %collective-permute-start.9 = (f32[26,8,128]{2,1,0:T(8,128)S(1)}, f32[26,8,128]{2,1,0:T(8,128)S(1)}, u32[]{:S(2)}, u32[]{:S(2)}) collective-permute-start(f32[26,8,128]{2,1,0:T(8,128)S(1)} %get-tuple-element.31), channel_id=1, source_target_pairs={{0,448},{32,480},{64,0},{96,32},{128,64},{160,96},{192,128},{224,1... | collective-permute-start | bytes 319496 | tf_op jit(solution)/shard_map/ppermute | solution.py:62
  60.8 2.8 %collective-permute-done.9.far_down = f32[26,8,128]{2,1,0:T(8,128)S(1)} collective-permute-done((f32[26,8,128]{2,1,0:T(8,128)S(1)}, f32[26,8,128]{2,1,0:T(8,128)S(1)}, u32[]{:S(2)}, u32[]{:S(2)}) %collective-permute-start.9) | collective-permute-done | bytes 106528 | tf_op jit(solution)/shard_map/ppermute | solution.py:62
  63.6 0.8 shard_map.76
  64.4 6.6 %all-to-all-start = ((f32[4,17,8,128]{3,2,1,0:T(8,128)}), f32[4,17,8,128]{3,2,1,0:T(8,128)S(1)}, u32[]{:S(2)}, u32[]{:S(2)}) async-start(f32[4,17,8,128]{3,2,1,0:T(8,128)} %shard_map.76), calls=%async_computation | async-start | bytes 557056 | tf_op jit(solution)/shard_map/all_to_all | solution.py:171
  71.5 15.5 %all-to-all-done.windows = f32[4,17,8,128]{3,2,1,0:T(8,128)S(1)} async-done(((f32[4,17,8,128]{3,2,1,0:T(8,128)}), f32[4,17,8,128]{3,2,1,0:T(8,128)S(1)}, u32[]{:S(2)}, u32[]{:S(2)}) %all-to-all-start) | async-done | bytes 278560 | tf_op jit(solution)/shard_map/all_to_all | solution.py:171
  87.0 1.3 shard_map.77
  88.2 11.5 %all-to-all-start.1 = ((f32[704,1,128]{2,1,0:T(1,128)}), f32[704,1,128]{2,1,0:T(1,128)S(1)}, u32[]{:S(2)}, u32[]{:S(2)}) async-start(f32[704,1,128]{2,1,0:T(1,128)} %bitcast.45), calls=%async_computation.1 | async-start | bytes 720896 | tf_op jit(solution)/shard_map/all_to_all | solution.py:105
  99.7 0.6 fusion.75
  100.4 1.3 fusion.77
  101.7 0.7 compare_select_fusion.2
  102.4 18.9 %all-to-all-done.1 = f32[704,1,128]{2,1,0:T(1,128)S(1)} async-done(((f32[704,1,128]{2,1,0:T(1,128)}), f32[704,1,128]{2,1,0:T(1,128)S(1)}, u32[]{:S(2)}, u32[]{:S(2)}) %all-to-all-start.1) | async-done | bytes 360480 | tf_op jit(solution)/shard_map/all_to_all | solution.py:105
  121.9 10.2 %all-to-all-start.2 = ((f32[8,1,128]{2,1,0:T(1,128)}), f32[8,1,128]{2,1,0:T(1,128)S(1)}, u32[]{:S(2)}, u32[]{:S(2)}) async-start(f32[8,1,128]{2,1,0:T(1,128)} %bitcast.48), calls=%async_computation.2 | async-start | bytes 8192 | tf_op jit(solution)/shard_map/all_to_all | solution.py:105
  132.1 0.7 gather_fusion.1
  132.9 0.7 gather_fusion.2
  133.6 0.6 gather_fusion
  134.2 2.4 %all-to-all-done.2 = f32[8,1,128]{2,1,0:T(1,128)S(1)} async-done(((f32[8,1,128]{2,1,0:T(1,128)}), f32[8,1,128]{2,1,0:T(1,128)S(1)}, u32[]{:S(2)}, u32[]{:S(2)}) %all-to-all-start.2) | async-done | bytes 4128 | tf_op jit(solution)/shard_map/all_to_all | solution.py:105
  136.6 1.4 %shard_map.79 = (f32[2,6656]{1,0:T(2,128)}, f32[2,6656]{1,0:T(2,128)}, bf16[208,128]{1,0:T(8,128)(2,1)}) custom-call(s32[1]{0:T(128)} %bitcast.length, f32[8,128]{1,0:T(8,128)S(1)} %bitcast.90, f32[2,6656]{1,0:T(2,128)S(1)} %reshape.933.mine, f32[2,6656]{1,0:T(2,128)S(1)} %copy-done, f32[2,6656]{1,0:T(2,128)S(1)} %copy-done.1, f32[208,128]{1,0:T(8,128)S(1)} %gather_fusion.1, ...), custom_call_target="tpu_custom_call" | custom-call | tf_op jit(solution)/shard_map/pallas_call | solution.py:196
  (58 shorter events, 2.0 us)
Async XLA Ops:
  0.7 3.1 %copy-start = (f32[2,6656]{1,0:T(2,128)S(1)}, f32[2,6656]{1,0:T(2,128)}, u32[]{:S(2)}) copy-start(f32[2,6656]{1,0:T(2,128)} %params.1) | copy-start | bytes 159748
  0.7 3.1 %copy-start.1 = (f32[2,6656]{1,0:T(2,128)S(1)}, f32[2,6656]{1,0:T(2,128)}, u32[]{:S(2)}) copy-start(f32[2,6656]{1,0:T(2,128)} %momentum.1) | copy-start | bytes 159748
  4.0 14.5 %collective-permute-start.2 = (f32[108,8,128]{2,1,0:T(8,128)S(1)}, f32[108,8,128]{2,1,0:T(8,128)S(1)}, u32[]{:S(2)}, u32[]{:S(2)}) collective-permute-start(f32[108,8,128]{2,1,0:T(8,128)S(1)} %pad_maximum_fusion.3), channel_id=1, source_target_pairs={{0,8},{8,16},{16,24},{24,0},{1,9},{9,17},{17,25},{25,1},{2,10},{10... | collective-permute-start | bytes 1327112 | tf_op jit(solution)/shard_map/ppermute | solution.py:38
  8.0 9.6 %collective-permute-start.3 = (f32[104,8,128]{2,1,0:T(8,128)}, f32[104,8,128]{2,1,0:T(8,128)S(1)}, u32[]{:S(2)}, u32[]{:S(2)}) collective-permute-start(f32[104,8,128]{2,1,0:T(8,128)} %bitcast.24), channel_id=1, source_target_pairs={{0,24},{8,0},{16,8},{24,16},{1,25},{9,1},{17,9},{25,17},{2,26},{10... | collective-permute-start | bytes 1277960 | tf_op jit(solution)/shard_map/ppermute | solution.py:39
  11.5 15.1 %collective-permute-start.1 = (f32[108,8,128]{2,1,0:T(8,128)S(1)}, f32[108,8,128]{2,1,0:T(8,128)S(1)}, u32[]{:S(2)}, u32[]{:S(2)}) collective-permute-start(f32[108,8,128]{2,1,0:T(8,128)S(1)} %pad_maximum_fusion.2), channel_id=1, source_target_pairs={{0,24},{8,0},{16,8},{24,16},{1,25},{9,1},{17,9},{25,17},{2,26},{10... | collective-permute-start | bytes 1327112 | tf_op jit(solution)/shard_map/ppermute | solution.py:42
  15.7 10.9 %collective-permute-start = (f32[108,8,128]{2,1,0:T(8,128)}, f32[108,8,128]{2,1,0:T(8,128)S(1)}, u32[]{:S(2)}, u32[]{:S(2)}) collective-permute-start(f32[108,8,128]{2,1,0:T(8,128)} %pad_maximum_fusion.1), channel_id=1, source_target_pairs={{0,8},{8,16},{16,24},{24,0},{1,9},{9,17},{17,25},{25,1},{2,10},{10... | collective-permute-start | bytes 1327112 | tf_op jit(solution)/shard_map/ppermute | solution.py:41
  18.6 17.5 %collective-permute-start.4 = (f32[108,8,128]{2,1,0:T(8,128)S(1)}, f32[108,8,128]{2,1,0:T(8,128)S(1)}, u32[]{:S(2)}, u32[]{:S(2)}) collective-permute-start(f32[108,8,128]{2,1,0:T(8,128)S(1)} %pad_maximum_fusion.4), channel_id=1, source_target_pairs={{0,8},{8,16},{16,24},{24,0},{1,9},{9,17},{17,25},{25,1},{2,10},{10... | collective-permute-start | bytes 1327112 | tf_op jit(solution)/shard_map/ppermute | solution.py:46
  24.6 11.4 %collective-permute-start.5 = (f32[104,8,128]{2,1,0:T(8,128)}, f32[104,8,128]{2,1,0:T(8,128)}, u32[]{:S(2)}, u32[]{:S(2)}) collective-permute-start(f32[104,8,128]{2,1,0:T(8,128)} %bitcast_add_fusion), channel_id=1, source_target_pairs={{0,24},{8,0},{16,8},{24,16},{1,25},{9,1},{17,9},{25,17},{2,26},{10... | collective-permute-start | bytes 1277960 | tf_op jit(solution)/shard_map/ppermute | solution.py:47
  37.4 33.5 %copy-start.2 = (s32[64]{0:T(128)S(1)}, s32[64]{0:T(128)}, u32[]{:S(2)}) copy-start(s32[64]{0:T(128)} %param.8) | copy-start | bytes 772
  37.5 33.5 %copy-start.3 = (s32[64]{0:T(128)S(1)}, s32[64]{0:T(128)}, u32[]{:S(2)}) copy-start(s32[64]{0:T(128)} %param.9) | copy-start | bytes 772
  37.7 25.9 %collective-permute-start.7 = (f32[56,8,128]{2,1,0:T(8,128)S(1)}, f32[56,8,128]{2,1,0:T(8,128)S(1)}, u32[]{:S(2)}, u32[]{:S(2)}) collective-permute-start(f32[56,8,128]{2,1,0:T(8,128)S(1)} %pad_maximum_fusion.6), channel_id=1, source_target_pairs={{0,480},{32,0},{64,32},{96,64},{128,96},{160,128},{192,160},{224,1... | collective-permute-start | bytes 688136 | tf_op jit(solution)/shard_map/ppermute | solution.py:64
  51.5 12.1 %collective-permute-start.6 = (f32[56,8,128]{2,1,0:T(8,128)S(1)}, f32[56,8,128]{2,1,0:T(8,128)S(1)}, u32[]{:S(2)}, u32[]{:S(2)}) collective-permute-start(f32[56,8,128]{2,1,0:T(8,128)S(1)} %pad_maximum_fusion.5), channel_id=1, source_target_pairs={{0,32},{32,64},{64,96},{96,128},{128,160},{160,192},{192,224},{224... | collective-permute-start | bytes 688136 | tf_op jit(solution)/shard_map/ppermute | solution.py:63
  53.4 10.2 %collective-permute-start.8 = (f32[30,8,128]{2,1,0:T(8,128)S(1)}, f32[30,8,128]{2,1,0:T(8,128)S(1)}, u32[]{:S(2)}, u32[]{:S(2)}) collective-permute-start(f32[30,8,128]{2,1,0:T(8,128)S(1)} %pad_maximum_fusion.7), channel_id=1, source_target_pairs={{0,64},{32,96},{64,128},{96,160},{128,192},{160,224},{192,256},{22... | collective-permute-start | bytes 368648 | tf_op jit(solution)/shard_map/ppermute | solution.py:61
  55.3 8.2 %collective-permute-start.9 = (f32[26,8,128]{2,1,0:T(8,128)S(1)}, f32[26,8,128]{2,1,0:T(8,128)S(1)}, u32[]{:S(2)}, u32[]{:S(2)}) collective-permute-start(f32[26,8,128]{2,1,0:T(8,128)S(1)} %get-tuple-element.31), channel_id=1, source_target_pairs={{0,448},{32,480},{64,0},{96,32},{128,64},{160,96},{192,128},{224,1... | collective-permute-start | bytes 319496 | tf_op jit(solution)/shard_map/ppermute | solution.py:62
  64.4 22.6 %all-to-all-start = ((f32[4,17,8,128]{3,2,1,0:T(8,128)}), f32[4,17,8,128]{3,2,1,0:T(8,128)S(1)}, u32[]{:S(2)}, u32[]{:S(2)}) async-start(f32[4,17,8,128]{3,2,1,0:T(8,128)} %shard_map.76), calls=%async_computation | async-start | bytes 557056 | tf_op jit(solution)/shard_map/all_to_all | solution.py:171
  88.2 33.1 %all-to-all-start.1 = ((f32[704,1,128]{2,1,0:T(1,128)}), f32[704,1,128]{2,1,0:T(1,128)S(1)}, u32[]{:S(2)}, u32[]{:S(2)}) async-start(f32[704,1,128]{2,1,0:T(1,128)} %bitcast.45), calls=%async_computation.1 | async-start | bytes 720896 | tf_op jit(solution)/shard_map/all_to_all | solution.py:105
  121.9 14.7 %all-to-all-start.2 = ((f32[8,1,128]{2,1,0:T(1,128)}), f32[8,1,128]{2,1,0:T(1,128)S(1)}, u32[]{:S(2)}, u32[]{:S(2)}) async-start(f32[8,1,128]{2,1,0:T(1,128)} %bitcast.48), calls=%async_computation.2 | async-start | bytes 8192 | tf_op jit(solution)/shard_map/all_to_all | solution.py:105
